TPU v7x, 256 devices: a whole 4x4x8 slice. The times are simulated.
256 devices in a mesh: seq: 4 (over z_hi), expert: 64 (over z_lo, y, x, core).
Axes of the slice: x: 4, y: 4, z: 8 (z_hi: 4, z_lo: 2; z = z_hi * 2 + z_lo), core: 2. Of those that a mesh axis runs over, the one named last changes fastest.
Arguments:
- tokens: bfloat16 [32768, 4096], P(('seq', 'expert')), may hold values from -6 to 6
- expert_ids: int32 [32768, 1], P(('seq', 'expert')), may hold values from 0 to 63; in each aligned block of 128 rows (0 to 127, 128 to 255, ...) at most 3 rows name the same one
- gate_weights: bfloat16 [32768, 1], P(('seq', 'expert')), may hold values from 0.049804688 to 1
- w_gate: bfloat16 [64, 768, 4096], P('expert', 'seq'), may hold values from -0.09375 to 0.09375
- w_up: bfloat16 [64, 768, 4096], P('expert', 'seq'), may hold values from -0.09375 to 0.09375
- w_down: bfloat16 [64, 768, 4096], P('expert', 'seq'), may hold values from -0.21875 to 0.21875
- cotangent: bfloat16 [32768, 4096], P(('seq', 'expert')), may hold values from -2 to 2
Outputs:
- d_tokens: bfloat16 [32768, 4096], P(('seq', 'expert'))
- d_gates: float32 [32768, 1], P(('seq', 'expert'))
- grad_gate: bfloat16 [64, 768, 4096], P('expert', 'seq')
- grad_up: bfloat16 [64, 768, 4096], P('expert', 'seq')
- grad_down: bfloat16 [64, 768, 4096], P('expert', 'seq')
Inputs may be any that keep to these rules, and one draw needn't show every extreme that they name: `expert_ids`: each row names one expert. Among the rows of one device (aligned blocks of 128 rows) no expert is named more than 3 times, and in every draw some expert is named exactly 3 times in some block.
All inputs are finite; a program needn't handle non-finite values.
Results may differ from a plain program's by a relative error of at most 0.012.
Values may be sent and summed in bfloat16 or wider, within the bound.
No kernel may reach another device: no remote copies, remote signals or barrier semaphores. Data moves between devices by JAX's collectives and lax.ppermute only.
A program may use at most 192 MiB of HBM per device.

v0:
```python
import jax
import jax.numpy as jnp
from jax import lax
from jax.sharding import PartitionSpec as P


def pair_slots(route_ids, capacity, experts):
    flat_ids = route_ids.reshape(1, -1)
    onehot = (flat_ids[:, :, None] == lax.iota(jnp.int32, experts)[None, None, :]).astype(jnp.int32)
    earlier = jnp.cumsum(onehot, axis=1) - onehot
    rank_in = jnp.sum(earlier * onehot, axis=2)
    return (flat_ids * capacity + rank_in).reshape(-1)


def scatter_rows(slot_index, rows_x, rows_dy, rows_gate, total_slots, top_count):
    pair_count = slot_index.shape[0]
    token_of = lax.iota(jnp.int32, pair_count) // top_count
    model_width = rows_x.shape[1]
    send_x = (
        jnp.zeros((total_slots, model_width), rows_x.dtype).at[slot_index].set(rows_x[token_of])
    )
    send_dy = (
        jnp.zeros((total_slots, model_width), rows_dy.dtype).at[slot_index].set(rows_dy[token_of])
    )
    send_gate = jnp.zeros((total_slots,), rows_gate.dtype).at[slot_index].set(rows_gate.reshape(-1))
    return (send_x, send_dy, send_gate)


def expert_terms(x_rows, dy_rows, gate_rows, gate_matrix, up_matrix, down_matrix):
    pre_gate = jnp.einsum("sd,hd->sh", x_rows, gate_matrix, preferred_element_type=jnp.float32)
    pre_up = jnp.einsum("sd,hd->sh", x_rows, up_matrix, preferred_element_type=jnp.float32)
    back = jnp.einsum("sd,hd->sh", dy_rows, down_matrix, preferred_element_type=jnp.float32)
    sigmoid_gate = jax.nn.sigmoid(pre_gate)
    silu_gate = pre_gate * sigmoid_gate
    activated = silu_gate * pre_up
    route_part = jnp.sum(activated * back, axis=1).astype(jnp.bfloat16)
    gate_col = gate_rows.astype(jnp.float32)[:, None]
    scaled = (gate_col * activated).astype(jnp.bfloat16)
    gated_back = gate_col * back
    grad_pre_gate = (
        gated_back * pre_up * sigmoid_gate * (1.0 + pre_gate * (1.0 - sigmoid_gate))
    ).astype(jnp.bfloat16)
    grad_pre_up = (gated_back * silu_gate).astype(jnp.bfloat16)
    token_part = (
        jnp.dot(grad_pre_gate, gate_matrix, preferred_element_type=jnp.float32)
        + jnp.dot(grad_pre_up, up_matrix, preferred_element_type=jnp.float32)
    ).astype(jnp.bfloat16)
    grad_gate = jnp.einsum("sh,sd->hd", grad_pre_gate, x_rows, preferred_element_type=jnp.float32)
    grad_up = jnp.einsum("sh,sd->hd", grad_pre_up, x_rows, preferred_element_type=jnp.float32)
    grad_down = jnp.einsum("sh,sd->hd", scaled, dy_rows, preferred_element_type=jnp.float32)
    return (token_part, route_part, grad_gate, grad_up, grad_down)


def run_experts(x_rows, dy_rows, gate_rows, gate_matrix, up_matrix, down_matrix):
    return expert_terms(x_rows, dy_rows, gate_rows, gate_matrix, up_matrix, down_matrix)


def per_device(tokens, expert_ids, gate_weights, w_gate, w_up, w_down, cotangent):
    experts = lax.axis_size("expert")
    groups = lax.axis_size("seq")
    tok_dev, model_width = tokens.shape
    top_count = expert_ids.shape[1]
    capacity = max(2, 3 * tok_dev * top_count // (2 * experts))
    per_expert = groups * capacity
    gate_matrix = w_gate[0]
    up_matrix = w_up[0]
    down_matrix = w_down[0]
    slot_index = pair_slots(expert_ids, capacity, experts)
    send_x, send_dy, send_gate = scatter_rows(
        slot_index, tokens, cotangent, gate_weights, experts * capacity, top_count
    )
    mine_x, mine_dy, mine_gate = (
        lax.all_to_all(
            send_x.reshape(experts, capacity, model_width),
            "expert",
            split_axis=0,
            concat_axis=0,
            tiled=True,
        ),
        lax.all_to_all(
            send_dy.reshape(experts, capacity, model_width),
            "expert",
            split_axis=0,
            concat_axis=0,
            tiled=True,
        ),
        lax.all_to_all(
            send_gate.reshape(experts, capacity), "expert", split_axis=0, concat_axis=0, tiled=True
        ),
    )
    group_x, group_dy, group_gate = (
        lax.all_gather(mine_x, "seq", axis=1, tiled=True),
        lax.all_gather(mine_dy, "seq", axis=1, tiled=True),
        lax.all_gather(mine_gate, "seq", axis=1, tiled=True),
    )
    outcome = run_experts(
        group_x.reshape(-1, model_width),
        group_dy.reshape(-1, model_width),
        group_gate.reshape(-1),
        gate_matrix,
        up_matrix,
        down_matrix,
    )
    token_parts = outcome[0]
    route_parts = outcome[1]
    grad_gate_sum = outcome[2]
    grad_up_sum = outcome[3]
    grad_down_sum = outcome[4]
    summed_tokens, summed_route = (
        lax.psum_scatter(
            token_parts.reshape(experts, per_expert, model_width)
            .astype(jnp.float32)
            .astype(jnp.bfloat16),
            "seq",
            scatter_dimension=1,
            tiled=True,
        ).astype(jnp.float32),
        lax.psum_scatter(
            route_parts.reshape(experts, per_expert).astype(jnp.float32).astype(jnp.bfloat16),
            "seq",
            scatter_dimension=1,
            tiled=True,
        ).astype(jnp.float32),
    )
    back_tokens, back_route = (
        lax.all_to_all(
            summed_tokens.astype(jnp.bfloat16), "expert", split_axis=0, concat_axis=0, tiled=True
        ).astype(summed_tokens.dtype),
        lax.all_to_all(
            summed_route.astype(jnp.bfloat16), "expert", split_axis=0, concat_axis=0, tiled=True
        ).astype(summed_route.dtype),
    )
    pair_tokens = back_tokens.reshape(-1, model_width)[slot_index].reshape(
        tok_dev, top_count, model_width
    )
    d_tokens = jnp.sum(pair_tokens, axis=1).astype(jnp.bfloat16)
    d_gates = back_route.reshape(-1)[slot_index].reshape(tok_dev, top_count)
    grad_gate = grad_gate_sum.astype(jnp.bfloat16)[None]
    grad_up = grad_up_sum.astype(jnp.bfloat16)[None]
    grad_down = grad_down_sum.astype(jnp.bfloat16)[None]
    return (d_tokens, d_gates, grad_gate, grad_up, grad_down)


def solution(mesh):
    placed = (
        P(("seq", "expert"), None),
        P(("seq", "expert"), None),
        P(("seq", "expert"), None),
        P("expert", "seq", None),
        P("expert", "seq", None),
        P("expert", "seq", None),
        P(("seq", "expert"), None),
    )
    return jax.shard_map(
        per_device,
        mesh=mesh,
        in_specs=placed,
        out_specs=(
            P(("seq", "expert"), None),
            P(("seq", "expert"), None),
            P("expert", "seq", None),
            P("expert", "seq", None),
            P("expert", "seq", None),
        ),
        check_vma=False,
    )
```

profile of v0, /device:TPU:1, one launch (start us, length us, event | category | flops | bytes accessed | tf_op | source)
XLA Modules:
  0.0 554.8 jit_solution(15842418678875918168)
XLA Ops:
  7.2 0.0 copy-start
  7.2 0.0 all-gather.4.cloned.1.call-start
  7.3 0.8 fusion.21
  8.1 0.2 reduce_window_sum.11
  8.3 0.8 select_reduce_fusion
  9.1 0.7 fusion.22
  9.8 5.5 scatter_custom_fusion.1
  15.3 2.3 reshape.166
  17.6 38.0 %all_to_all.37 = bf16[64,3,4096]{2,1,0:T(4,128)(2,1)S(1)} all-to-all(bf16[64,3,4096]{2,1,0:T(4,128)(2,1)} %reshape.166), channel_id=1, replica_groups=mesh['seq'=4,'expert'=64] {'expert'}, dimensions={0} | all-to-all | bytes 3145728 | tf_op jit(solution)/shard_map/all_to_all | solution.py:80
  55.6 2.3 copy.25
  57.9 0.0 all-gather.4.cloned.1.call-update
  57.9 0.0 all-gather.6.cloned.1.call-start
  57.9 5.6 %scatter_custom_fusion.2 = bf16[192,4096]{1,0:T(8,128)(2,1)S(1)} fusion(s32[128]{0:T(128)S(1)} %fusion.22, bf16[128,4096]{1,0:T(8,128)(2,1)} %param.7, s32[1024]{0:T(1024)S(1)} %pad_clamp_fusion.1, bf16[]{:T(256)} %constant.13.clone.1), kind=kCustom, calls=%fused_computation.23 | custom fusion | bytes 1573376 | tf_op jit(solution)/shard_map/scatter | solution.py:20
  63.6 2.3 reshape.168
  65.9 92.0 %all_to_all.38 = bf16[64,3,4096]{2,1,0:T(4,128)(2,1)S(1)} all-to-all(bf16[64,3,4096]{2,1,0:T(4,128)(2,1)} %reshape.168), channel_id=1, replica_groups=mesh['seq'=4,'expert'=64] {'expert'}, dimensions={0} | all-to-all | bytes 3145728 | tf_op jit(solution)/shard_map/all_to_all | solution.py:73
  157.9 2.3 copy.27
  160.2 0.0 all-gather.6.cloned.1.call-update
  160.2 0.0 reduce-scatter.3.cloned.1.call-start
  160.2 1.5 scatter_custom_fusion
  161.7 0.2 all_to_all.31
  161.9 22.3 %all_to_all.39 = bf16[64,1,3]{2,1,0:T(2,128)(2,1)S(1)} all-to-all(bf16[64,1,3]{2,1,0:T(2,128)(2,1)S(1)} %all_to_all.31), channel_id=1, replica_groups=mesh['seq'=4,'expert'=64] {'expert'}, dimensions={0} | all-to-all | bytes 768 | tf_op jit(solution)/shard_map/all_to_all | solution.py:87
  184.2 0.1 copy.23
  184.3 32.6 %all-gather = bf16[64,1,12]{0,1,2:T(2,128)(2,1)S(1)} all-gather(bf16[64,1,3]{0,1,2:T(2,128)(2,1)S(1)} %copy.23), channel_id=2, replica_groups=mesh['seq'=4,'expert'=64] {'seq'}, dimensions={2}, use_global_device_ids=true | all-gather | bytes 1920 | tf_op jit(solution)/shard_map/all_gather | solution.py:94
  216.9 0.1 copy.24
  217.0 0.1 reshape.174
  217.1 0.0 all-gather.4.cloned.1.call-done
  217.2 10.1 %copy.26 = bf16[64,12,4096]{2,1,0:T(8,128)(2,1)} copy(bf16[64,12,4096]{2,0,1:T(8,128)(2,1)} %all-gather.4.cloned.1.call-done) | data formatting | bytes 12582912 | tf_op jit(solution)/shard_map/all_gather | solution.py:93
  227.2 9.9 %reshape.167 = bf16[768,4096]{1,0:T(8,128)(2,1)} reshape(bf16[64,12,4096]{2,1,0:T(8,128)(2,1)} %copy.26) | data formatting | bytes 12582912 | tf_op jit(solution)/shard_map/reshape | solution.py:98
  237.1 80.6 %all-gather.6.cloned.1.call-done = bf16[64,12,4096]{2,0,1:T(8,128)(2,1)} async-done(((bf16[64,3,4096]{2,0,1:T(8,128)(2,1)}), bf16[64,12,4096]{2,0,1:T(8,128)(2,1)}) %all-gather.6.cloned.1.call-update) | async-done | bytes 6291472 | tf_op jit(solution)/shard_map/all_gather | solution.py:92
  317.7 9.6 %copy.28 = bf16[64,12,4096]{2,1,0:T(8,128)(2,1)} copy(bf16[64,12,4096]{2,0,1:T(8,128)(2,1)} %all-gather.6.cloned.1.call-done) | data formatting | bytes 12582912 | tf_op jit(solution)/shard_map/all_gather | solution.py:92
  327.3 10.1 %reshape.169 = bf16[768,4096]{1,0:T(8,128)(2,1)} reshape(bf16[64,12,4096]{2,1,0:T(8,128)(2,1)} %copy.28) | data formatting | bytes 12582912 | tf_op jit(solution)/shard_map/reshape | solution.py:97
  337.4 0.0 copy-start.2
  337.4 5.2 fusion.5
  342.6 0.0 copy-start.3
  342.6 5.2 fusion.8
  347.8 0.0 copy-start.5
  347.8 2.5 multiply_reduce_fusion
  350.4 1.8 fusion.3
  352.2 4.5 add_convert_fusion
  356.7 10.0 %reshape.170 = bf16[64,12,4096]{2,1,0:T(8,128)(2,1)} reshape(bf16[768,4096]{1,0:T(8,128)(2,1)} %add_convert_fusion) | data formatting | bytes 12582912 | tf_op jit(solution)/shard_map/reshape | solution.py:111
  366.7 9.5 %copy.29 = bf16[64,12,4096]{2,0,1:T(8,128)(2,1)} copy(bf16[64,12,4096]{2,1,0:T(8,128)(2,1)} %reshape.170) | data formatting | bytes 12582912 | tf_op jit(solution)/shard_map/reshape | solution.py:111
  376.2 0.0 reduce-scatter.3.cloned.1.call-update
  376.2 0.6 copy-done.4
  376.9 0.6 dynamic-slice
  378.1 0.1 convert_element_type.80
  378.2 23.0 %all-reduce = bf16[64,12]{1,0:T(8,128)(2,1)S(1)} all-reduce(bf16[64,12]{1,0:T(8,128)(2,1)S(1)} %convert_element_type.80), channel_id=4, replica_groups=mesh['seq'=4,'expert'=64] {'seq'}, use_global_device_ids=true, to_apply=%region_7.8.clone | all-reduce | flops 768 | bytes 3072
  401.2 0.1 dynamic-slice_bitcast_fusion
  401.3 0.6 copy.31
  401.9 11.8 %all-to-all-start.4 = ((bf16[64,1,3]{2,1,0:T(2,128)(2,1)}), bf16[64,1,3]{2,1,0:T(2,128)(2,1)S(1)}, u32[]{:S(2)}, u32[]{:S(2)}) async-start(bf16[64,1,3]{2,1,0:T(2,128)(2,1)} %copy.31), calls=%async_computation.5 | async-start | bytes 65536 | tf_op jit(solution)/shard_map/all_to_all | solution.py:129
  413.8 87.2 %reduce-scatter.3.cloned.1.call-done = bf16[64,3,4096]{2,0,1:T(8,128)(2,1)} async-done(((bf16[64,12,4096]{2,0,1:T(8,128)(2,1)}), bf16[64,3,4096]{2,0,1:T(8,128)(2,1)}) %reduce-scatter.3.cloned.1.call-update) | async-done | bytes 1572880 | tf_op jit(solution)/shard_map/reduce_scatter | solution.py:110
  501.0 4.1 copy.30
  505.1 0.0 all-to-all-done.4
  505.1 10.0 %all-to-all-start.3 = ((bf16[64,3,4096]{2,1,0:T(4,128)(2,1)}), bf16[64,3,4096]{2,1,0:T(4,128)(2,1)}, u32[]{:S(2)}, u32[]{:S(2)}) async-start(bf16[64,3,4096]{2,1,0:T(4,128)(2,1)} %copy.30), calls=%async_computation.4 | async-start | bytes 4194304 | tf_op jit(solution)/shard_map/all_to_all | solution.py:126
  515.1 0.0 slice-start.2
  515.1 5.5 fusion
  520.6 5.5 fusion.1
  526.1 2.7 fusion.2
  528.8 0.1 convert_reduce_fusion
  528.9 0.1 reshape.177
  529.0 1.8 gather_fusion.1
  530.8 11.7 %all-to-all-done.3 = bf16[64,3,4096]{2,1,0:T(4,128)(2,1)} async-done(((bf16[64,3,4096]{2,1,0:T(4,128)(2,1)}), bf16[64,3,4096]{2,1,0:T(4,128)(2,1)}, u32[]{:S(2)}, u32[]{:S(2)}) %all-to-all-start.3) | async-done | bytes 1572896 | tf_op jit(solution)/shard_map/all_to_all | solution.py:126
  542.5 3.1 reshape.176
  545.6 0.0 copy-start.1
  545.6 2.2 gather_fusion
  (20 shorter events, 0.0 us)
Async XLA Ops:
  7.2 330.2 %copy-start = (bf16[1,192,4096]{2,1,0:T(8,128)(2,1)S(1)}, bf16[1,192,4096]{2,1,0:T(8,128)(2,1)}, u32[]{:S(2)}) copy-start(bf16[1,192,4096]{2,1,0:T(8,128)(2,1)} %param.10) | copy-start | bytes 4718596
  7.2 210.0 %all-gather.4.cloned.1.call-start = ((), (), s32[]{:S(2)}) async-start(), calls=%async_computation.6 | async-start | bytes 7864320 | tf_op jit(solution)/shard_map/all_gather | solution.py:93
  57.9 259.8 %all-gather.6.cloned.1.call-start = ((), (), s32[]{:S(2)}) async-start(), calls=%async_computation.7 | async-start | bytes 7864320 | tf_op jit(solution)/shard_map/all_gather | solution.py:92
  160.2 340.8 %reduce-scatter.3.cloned.1.call-start = ((), (), s32[]{:S(2)}) async-start(), calls=%async_computation.8 | async-start | bytes 7864320 | tf_op jit(solution)/shard_map/reduce_scatter | solution.py:110
  337.4 5.2 copy-start.2
  337.4 10.4 %slice-start = ((s8[6291456]{0:T(1024)(128)(4,1)}), s8[4194304]{0:T(1024)(128)(4,1)S(1)}, s32[]{:S(2)}) async-start(s8[6291456]{0:T(1024)(128)(4,1)} %bitcast.50), calls=%async_computation.9 | async-start | bytes 8388608
  342.6 5.2 slice-start.1
  342.6 5.2 copy-start.3
  347.8 2.5 copy-start.5
  376.2 0.7 copy-start.4
  401.9 103.1 %all-to-all-start.4 = ((bf16[64,1,3]{2,1,0:T(2,128)(2,1)}), bf16[64,1,3]{2,1,0:T(2,128)(2,1)S(1)}, u32[]{:S(2)}, u32[]{:S(2)}) async-start(bf16[64,1,3]{2,1,0:T(2,128)(2,1)} %copy.31), calls=%async_computation.5 | async-start | bytes 65536 | tf_op jit(solution)/shard_map/all_to_all | solution.py:129
  505.1 37.4 %all-to-all-start.3 = ((bf16[64,3,4096]{2,1,0:T(4,128)(2,1)}), bf16[64,3,4096]{2,1,0:T(4,128)(2,1)}, u32[]{:S(2)}, u32[]{:S(2)}) async-start(bf16[64,3,4096]{2,1,0:T(4,128)(2,1)} %copy.30), calls=%async_computation.4 | async-start | bytes 4194304 | tf_op jit(solution)/shard_map/all_to_all | solution.py:126
  515.1 11.0 %slice-start.2 = ((s8[6291456]{0:T(1024)(128)(4,1)}), s8[4194304]{0:T(1024)(128)(4,1)S(1)}, s32[]{:S(2)}) async-start(s8[6291456]{0:T(1024)(128)(4,1)} %bitcast.52), calls=%async_computation.11 | async-start | bytes 8388608
  520.6 5.5 slice-start.3
  520.6 5.5 copy-start.6
  545.6 2.2 copy-start.1
Sparse Core Ops, SparseCore 0:
  58.0 144.4 all-gather.3
  204.9 112.7 all-gather.5
  376.3 124.5 reduce-scatter.2
where the time goes:
time: 565 us; the launch traced here: 555 us
  blocking collectives  208 us (37%)
  waiting for transfers between devices  180 us (32%)
  local copies, waits for them, and re-layouts  94.8 us (17%)
  matrix products  32.8 us (6%)
  starting transfers between devices  22 us (4%)
  between operations  15.2 us (3%)
    all_to_all x1, blocking collectives, per_device(): lax.all_to_all(send_x.reshape(experts, capacity, model_width), 'expert',...  92 us
    reduce_scatter x1, waiting for transfers between devices, per_device(): lax.psum_scatter(token_parts.reshape(experts, per_expert, model_width).as...  87.2 us
    all_gather x1, waiting for transfers between devices, per_device(): lax.all_gather(mine_x, 'seq', axis=1, tiled=True)  80.6 us
    all_to_all x1, blocking collectives, per_device(): lax.all_to_all(send_dy.reshape(experts, capacity, model_width), 'expert',...  38 us
    all_gather x1, blocking collectives, per_device(): lax.all_gather(mine_gate, 'seq', axis=1, tiled=True)  32.6 us
    unnamed x1, blocking collectives  23 us
    all_to_all x1, blocking collectives, per_device(): lax.all_to_all(send_gate.reshape(experts, capacity), 'expert', split_axis...  22.3 us
    reshape x2, local copies, waits for them, and re-layouts, per_device(): token_parts.reshape(experts, per_expert, model_width).astype(jnp.float32)  19.5 us
  transfers between devices with their start and end apart: 5, of which 3 were waited for; matrix products, arithmetic and copies ran while one was open for 10% of the time, Pallas kernels for 0%

commit v1 on v0

v1 whole, which is shorter than its diff:
```python
import jax
import jax.numpy as jnp
import numpy as np
from jax import lax
from jax.sharding import Mesh, PartitionSpec as P

CAP = 3
ZLO = 2
LANES = 128
COLUMN = ("seq", "zlo")
PLANE = ("y", "x", "core")
EXPERT = ("zlo", "y", "x", "core")
BF = jnp.bfloat16
F32 = jnp.float32


def dot(a, b, out=F32):
    return lax.dot_general(a, b, (((1,), (0,)), ((), ())), preferred_element_type=out)


def dot_t(a, b, out=F32):
    return lax.dot_general(a, b, (((1,), (1,)), ((), ())), preferred_element_type=out)


def tdot(a, b, out=F32):
    return lax.dot_general(a, b, (((0,), (0,)), ((), ())), preferred_element_type=out)


def column_gather(values, depth, me):
    got = [values]
    for far in range(1, depth):
        got.append(lax.ppermute(values, COLUMN, [(i, (i + far) % depth) for i in range(depth)]))
    picked = lax.rem(me - lax.iota(jnp.int32, depth) + depth, depth)
    return jnp.take(jnp.stack(got), picked, axis=0)


def per_device(tokens, expert_ids, gate_weights, w_gate, w_up, w_down, cotangent):
    groups = lax.axis_size("seq")
    plane = lax.axis_size(PLANE)
    depth = groups * ZLO
    experts = plane * ZLO
    rows, width = tokens.shape
    half = width // 2
    send = experts * CAP
    held = send * groups
    block = depth * CAP
    zlo = lax.axis_index("zlo")
    me = lax.axis_index("seq") * ZLO + zlo
    wg, wu, wd = w_gate[0], w_up[0], w_down[0]

    ids = expert_ids[:, 0]
    here = lax.iota(jnp.int32, rows)
    same = (ids[:, None] == ids[None, :]) & (here[None, :] < here[:, None])
    rank = jnp.sum(same.astype(jnp.int32), axis=1)
    slot = ids * CAP + rank
    to_slot = (slot[None, :] == lax.iota(jnp.int32, send)[:, None]).astype(BF)
    from_slot = (slot[:, None] == lax.iota(jnp.int32, send)[None, :]).astype(BF)

    x_column = lax.all_gather(tokens, COLUMN, axis=0, tiled=True)

    dy_send = dot(to_slot, cotangent, BF).reshape(experts, CAP, width)
    dy_mine = lax.all_to_all(dy_send, EXPERT, 0, 0, tiled=True).reshape(send, width)
    dy_held = lax.all_gather(dy_mine, "seq", axis=0, tiled=True)

    code = (ids % plane) * block + me * CAP + rank + held * (ids // plane)
    meta = jnp.stack([code.astype(F32), gate_weights[:, 0].astype(F32)])
    meta = column_gather(meta, depth, me)
    target = meta[:, 0, :].reshape(-1).astype(jnp.int32) - held * zlo
    gates_column = meta[:, 1, :].reshape(-1)
    in_column = depth * rows
    hit = target[None, :] == lax.iota(jnp.int32, held)[:, None]
    pick = hit.astype(BF)
    unpick = (target[:, None] == lax.iota(jnp.int32, held)[None, :]).astype(BF)
    gate_send = jnp.sum(jnp.where(hit, gates_column[None, :], 0.0), axis=1).reshape(plane, block)
    gate_x = lax.all_to_all(gate_send, PLANE, 0, 0, tiled=True).reshape(held)

    x_send = dot(pick, x_column, BF).reshape(plane, block, width)
    x_held = lax.all_to_all(x_send, PLANE, 0, 0, tiled=True).reshape(held, width)

    at = lax.iota(jnp.int32, held)
    as_x = (at % (plane * CAP)) // CAP * block + at // (plane * CAP) * CAP + at % CAP
    turn = as_x[:, None] == at[None, :]
    turn_bf = turn.astype(BF)
    turn_f32 = turn.astype(F32)
    pre_x = jnp.concatenate([dot_t(x_held, wg), dot_t(x_held, wu)], axis=1)
    pre = lax.dot_general(
        turn_f32, pre_x, (((1,), (0,)), ((), ())), precision=lax.Precision.HIGHEST,
        preferred_element_type=F32,
    )
    hidden = wg.shape[0]
    pre_gate, pre_up = pre[:, :hidden], pre[:, hidden:]
    gate_col = jnp.sum(jnp.where(turn, gate_x[None, :], 0.0), axis=1)[:, None]

    back = dot_t(dy_held, wd)
    sigmoid_gate = jax.nn.sigmoid(pre_gate)
    silu_gate = pre_gate * sigmoid_gate
    activated = silu_gate * pre_up
    route = jnp.sum(activated * back, axis=1, keepdims=True).astype(BF)
    scaled = (gate_col * activated).astype(BF)
    gated_back = gate_col * back
    g_gate = (gated_back * pre_up * sigmoid_gate * (1.0 + pre_gate * (1.0 - sigmoid_gate))).astype(BF)
    g_up = (gated_back * silu_gate).astype(BF)

    part_a = (dot(g_gate, wg[:, :half]) + dot(g_up, wu[:, :half])).astype(BF)
    sum_a = lax.psum_scatter(part_a, "seq", scatter_dimension=0, tiled=True)

    g_gate_x = tdot(turn_bf, g_gate, BF)
    g_up_x = tdot(turn_bf, g_up, BF)
    route_x = tdot(turn_bf, jnp.broadcast_to(route, (held, LANES)), BF)
    part_b = (dot(g_gate_x, wg[:, half:]) + dot(g_up_x, wu[:, half:])).astype(BF)
    part_b = jnp.concatenate([part_b, route_x], axis=1)
    back_b = lax.all_to_all(part_b.reshape(plane, block, half + LANES), PLANE, 0, 0, tiled=True)
    column_b = dot(unpick, back_b.reshape(held, half + LANES), BF)
    sum_b = lax.psum_scatter(column_b, COLUMN, scatter_dimension=0, tiled=True)

    back_a = lax.all_to_all(sum_a.reshape(experts, CAP, half), EXPERT, 0, 0, tiled=True)
    rows_a = dot(from_slot, back_a.reshape(send, half), BF)

    grad_gate = tdot(g_gate_x, x_held, BF)
    grad_up = tdot(g_up_x, x_held, BF)
    grad_down = tdot(scaled, dy_held, BF)

    d_tokens = jnp.concatenate([rows_a, sum_b[:, :half]], axis=1)
    d_gates = sum_b[:, half:half + 1].astype(F32)
    return (d_tokens, d_gates, grad_gate[None], grad_up[None], grad_down[None])


def solution(mesh):
    groups, experts = mesh.shape["seq"], mesh.shape["expert"]
    side = int(np.sqrt(experts // (2 * ZLO)))
    fine = Mesh(
        np.asarray(mesh.devices).reshape(groups, ZLO, experts // (2 * ZLO * side), side, 2),
        ("seq", "zlo", "y", "x", "core"),
    )
    by_row = P(("seq",) + EXPERT, None)
    by_expert = P(EXPERT, "seq", None)
    return jax.shard_map(
        per_device,
        mesh=fine,
        in_specs=(by_row, by_row, by_row, by_expert, by_expert, by_expert, by_row),
        out_specs=(by_row, by_row, by_expert, by_expert, by_expert),
        check_vma=False,
    )
```

time: 565 us -> 408 us (0.72); the launches traced: 555 us -> 407 us
  blocking collectives: 208 us -> 55.3 us
  local copies, waits for them, and re-layouts: 94.8 us -> 14.7 us
  starting transfers between devices: 22 us -> 56.3 us
  matrix products: 32.8 us -> 61.8 us
  waiting for transfers between devices: 180 us -> 199 us
    all_to_all x3 -> x1, blocking collectives: 152 us -> 55.3 us  [per_device(): lax.all_to_all(part_b.reshape(plane, block, half + LANES), PLANE, 0, 0, t...]
    all_to_all x2 -> x4, waiting for transfers between devices: 11.7 us -> 84.4 us  [the longest x1 71.1 us: per_device(): lax.all_to_all(x_send, PLANE, 0, 0, tiled=True).reshape(held, width)]
    reduce_scatter x1 -> x2, waiting for transfers between devices: 87.2 us -> 34.8 us  [the longest x1 28.3 us: per_device(): sum_b = lax.psum_scatter(column_b, COLUMN, scatter_dimension=0, tiled=True)]
    reshape x7 -> x4, local copies, waits for them, and re-layouts: 47.2 us -> 10.5 us  [the longest x1 4.27 us: per_device(): lax.all_to_all(dy_send, EXPERT, 0, 0, tiled=True).reshape(send, width)]
    all_gather x2, waiting for transfers between devices: 80.6 us -> 44.4 us  [the longest x1 33.2 us: per_device(): x_column = lax.all_gather(tokens, COLUMN, axis=0, tiled=True)]
    ppermute x0 -> x7, waiting for transfers between devices: none -> 34.9 us  [column_gather(): lax.ppermute(values, COLUMN, [(i, (i + far) % depth) for i in range(depth)])]
    all_gather x1 -> x0, blocking collectives: 32.6 us -> none  [per_device(): lax.all_gather(mine_gate, 'seq', axis=1, tiled=True)]
    dot_general x8 -> x18, matrix products: 32.8 us -> 61.8 us  [the longest x8 25.4 us: dot(): lax.dot_general(a, b, (((1,), (0,)), ((), ())), preferred_element_type=out)]
  transfers between devices with their start and end apart: 5 -> 15, of which waited for: 3 -> 9; matrix products, arithmetic and copies ran while one was open for 10% -> 17% of each run, Pallas kernels for 0% -> 0%
where the time goes in v1:
time: 408 us; the launch traced here: 407 us
  waiting for transfers between devices  199 us (49%)
  matrix products  61.8 us (15%)
  starting transfers between devices  56.3 us (14%)
  blocking collectives  55.3 us (14%)
  local copies, waits for them, and re-layouts  14.7 us (4%)
  between operations  14.2 us (3%)
  other arithmetic  5.4 us (1%)
    all_to_all x1, waiting for transfers between devices, per_device(): lax.all_to_all(x_send, PLANE, 0, 0, tiled=True).reshape(held, width)  71.1 us
    all_to_all x1, blocking collectives, per_device(): lax.all_to_all(part_b.reshape(plane, block, half + LANES), PLANE, 0, 0, t...  55.3 us
    ppermute x7, waiting for transfers between devices, column_gather(): lax.ppermute(values, COLUMN, [(i, (i + far) % depth) for i in range(depth)])  34.9 us
    all_gather x1, waiting for transfers between devices, per_device(): x_column = lax.all_gather(tokens, COLUMN, axis=0, tiled=True)  33.2 us
    reduce_scatter x1, waiting for transfers between devices, per_device(): sum_b = lax.psum_scatter(column_b, COLUMN, scatter_dimension=0, tiled=True)  28.3 us
    dot_general x8, matrix products, dot(): lax.dot_general(a, b, (((1,), (0,)), ((), ())), preferred_element_type=out)  25.4 us
    ppermute x7, starting transfers between devices, column_gather(): lax.ppermute(values, COLUMN, [(i, (i + far) % depth) for i in range(depth)])  20.2 us
    dot_general x6, matrix products, tdot(): lax.dot_general(a, b, (((0,), (0,)), ((), ())), preferred_element_type=out)  17.4 us
  transfers between devices with their start and end apart: 15, of which 9 were waited for; matrix products, arithmetic and copies ran while one was open for 17% of the time, Pallas kernels for 0%

profile of v1, /device:TPU:1, one launch (start us, length us, event | category | flops | bytes accessed | tf_op | source)
XLA Modules:
  0.0 406.8 jit_solution(1096296496318085417)
XLA Ops:
  7.2 0.0 all-gather.5.cloned.1.call-start
  7.2 0.7 all-gather.5.cloned.1.call-update
  7.9 0.9 convert_reduce_fusion
  8.8 0.7 multiply_add_fusion
  9.5 1.8 fusion.27
  11.3 2.3 reshape.278
  13.6 10.5 %all-to-all-start.1 = ((bf16[64,3,4096]{2,1,0:T(4,128)(2,1)}), bf16[64,3,4096]{2,1,0:T(4,128)(2,1)}, u32[]{:S(2)}, u32[]{:S(2)}) async-start(bf16[64,3,4096]{2,1,0:T(4,128)(2,1)} %reshape.278), calls=%async_computation.1 | async-start | bytes 4194304 | tf_op jit(solution)/shard_map/all_to_all | solution.py:62
  24.2 0.0 all-gather.3.cloned.1.call-start
  24.3 5.2 %collective-permute-start.5 = (f32[2,128]{1,0:T(2,128)S(1)}, f32[2,128]{1,0:T(2,128)S(1)}, u32[]{:S(2)}, u32[]{:S(2)}) collective-permute-start(f32[2,128]{1,0:T(2,128)S(1)} %pad_maximum_fusion.2), channel_id=1, source_target_pairs={{0,192},{32,224},{64,0},{96,32},{128,64},{160,96},{192,128},{224,1... | collective-permute-start | bytes 3080 | tf_op jit(solution)/shard_map/ppermute | solution.py:32
  29.5 1.5 collective-permute-start.4
  30.9 4.2 %collective-permute-start.3 = (f32[2,128]{1,0:T(2,128)S(1)}, f32[2,128]{1,0:T(2,128)S(1)}, u32[]{:S(2)}, u32[]{:S(2)}) collective-permute-start(f32[2,128]{1,0:T(2,128)S(1)} %pad_maximum_fusion.2), channel_id=1, source_target_pairs={{0,128},{32,160},{64,192},{96,224},{128,0},{160,32},{192,64},{224,... | collective-permute-start | bytes 3080 | tf_op jit(solution)/shard_map/ppermute | solution.py:32
  35.2 1.4 collective-permute-start
  36.7 31.4 %collective-permute-done = f32[2,128]{1,0:T(2,128)S(1)} collective-permute-done((f32[2,128]{1,0:T(2,128)S(1)}, f32[2,128]{1,0:T(2,128)S(1)}, u32[]{:S(2)}, u32[]{:S(2)}) %collective-permute-start) | collective-permute-done | bytes 1056 | tf_op jit(solution)/shard_map/ppermute | solution.py:32
  68.0 4.3 %collective-permute-start.1 = (f32[2,128]{1,0:T(2,128)S(1)}, f32[2,128]{1,0:T(2,128)S(1)}, u32[]{:S(2)}, u32[]{:S(2)}) collective-permute-start(f32[2,128]{1,0:T(2,128)S(1)} %pad_maximum_fusion.2), channel_id=1, source_target_pairs={{0,64},{32,96},{64,128},{96,160},{128,192},{160,224},{192,0},{224,... | collective-permute-start | bytes 3080 | tf_op jit(solution)/shard_map/ppermute | solution.py:32
  72.4 2.9 collective-permute-done.1
  75.3 3.6 collective-permute-start.6
  78.9 0.6 collective-permute-done.6
  79.6 0.6 gather_fusion
  80.2 4.3 %reshape.279 = bf16[192,4096]{1,0:T(8,128)(2,1)} reshape(bf16[64,3,4096]{2,1,0:T(4,128)(2,1)} %all-to-all-done.1) | data formatting | bytes 3145728 | tf_op jit(solution)/shard_map/reshape | solution.py:62
  84.4 0.0 all-gather.3.cloned.1.call-update
  84.5 0.1 broadcast_select_fusion
  84.6 0.4 select_reduce_fusion
  85.0 0.7 all_to_all.18
  85.6 9.5 %all-to-all-start = ((f32[32,1,24]{2,1,0:T(1,128)}), f32[32,1,24]{2,1,0:T(1,128)S(1)}, u32[]{:S(2)}, u32[]{:S(2)}) async-start(f32[32,1,24]{2,1,0:T(1,128)} %bitcast.17), calls=%async_computation | async-start | bytes 32768 | tf_op jit(solution)/shard_map/all_to_all | solution.py:75
  95.2 33.2 %all-gather.5.cloned.1.call-done = bf16[1024,4096]{1,0:T(8,128)(2,1)} async-done(((bf16[128,4096]{1,0:T(8,128)(2,1)}), bf16[1024,4096]{1,0:T(8,128)(2,1)}) %all-gather.5.cloned.1.call-update) | async-done | bytes 8388624 | tf_op jit(solution)/shard_map/all_gather | solution.py:59
  128.4 11.8 %fusion = bf16[768,4096]{1,0:T(8,128)(2,1)} fusion(bf16[1024,4096]{1,0:T(8,128)(2,1)} %all-gather.5.cloned.1.call-done, s32[1024]{0:T(1024)S(1)} %bitcast.98), kind=kOutput, calls=%fused_computation.10 | convolution fusion | flops 6443237376 | bytes 14684160 | tf_op jit(solution)/shard_map/dot_general | solution.py:18
  140.2 7.6 %all-to-all-start.2 = ((bf16[32,24,4096]{2,1,0:T(8,128)(2,1)}), bf16[32,24,4096]{2,1,0:T(8,128)(2,1)}, u32[]{:S(2)}, u32[]{:S(2)}) async-start(bf16[32,24,4096]{2,1,0:T(8,128)(2,1)} %bitcast.91), calls=%async_computation.2 | async-start | bytes 12582912 | tf_op jit(solution)/shard_map/all_to_all | solution.py:78
  147.8 0.0 reduce-scatter.3.cloned.1.call-start
  147.9 0.5 broadcast.302
  148.4 0.7 reduce.3
  149.1 0.1 broadcast_in_dim.71
  149.2 0.5 select_reduce_fusion.1
  149.7 71.1 %all-to-all-done.2 = bf16[32,24,4096]{2,1,0:T(8,128)(2,1)} async-done(((bf16[32,24,4096]{2,1,0:T(8,128)(2,1)}), bf16[32,24,4096]{2,1,0:T(8,128)(2,1)}, u32[]{:S(2)}, u32[]{:S(2)}) %all-to-all-start.2) | async-done | bytes 6291488 | tf_op jit(solution)/shard_map/all_to_all | solution.py:78
  220.8 5.6 %fusion.64 = f32[768,192]{0,1:T(8,128)S(1)} fusion(bf16[768,4096]{1,0:T(8,128)(2,1)} %bitcast.20, bf16[1,192,4096]{2,1,0:T(8,128)(2,1)} %param.11), kind=kOutput, calls=%fused_computation.122 | convolution fusion | flops 1207959552 | bytes 8454144 | tf_op jit(solution)/shard_map/dot_general | solution.py:22
  226.4 5.0 %fusion.66 = f32[768,192]{0,1:T(8,128)S(1)} fusion(bf16[768,4096]{1,0:T(8,128)(2,1)} %bitcast.20, bf16[1,192,4096]{2,1,0:T(8,128)(2,1)S(1)} %copy-done.2), kind=kOutput, calls=%fused_computation.124 | convolution fusion | flops 1207959552 | bytes 8454144 | tf_op jit(solution)/shard_map/dot_general | solution.py:22
  231.4 2.9 fusion.5
  234.3 11.2 %all-gather.3.cloned.1.call-done = bf16[768,4096]{1,0:T(8,128)(2,1)} async-done(((bf16[192,4096]{1,0:T(8,128)(2,1)}), bf16[768,4096]{1,0:T(8,128)(2,1)}) %all-gather.3.cloned.1.call-update) | async-done | bytes 6291472 | tf_op jit(solution)/shard_map/all_gather | solution.py:63
  245.5 5.4 %multiply_convert_fusion.1 = (bf16[768,192]{0,1:T(8,128)(2,1)S(1)}, bf16[768,192]{0,1:T(8,128)(2,1)S(1)}, bf16[768]{0:T(1024)(128)(2,1)S(1)}) fusion(f32[768]{0:T(1024)S(1)} %select_reduce_fusion.1, f32[768,384]{0,1:T(8,128)} %fusion.5, bf16[768,4096]{1,0:T(8,128)(2,1)} %all-gather.3.cloned.1.call-done, bf16[1,192,4096]{2,1,0:T(8,128)(2,1)S(1)} %copy-done), kind=kOutput, calls=%fused_computation.38 | convolution fusion | flops 1210465536 | bytes 9638400 | tf_op jit(solution)/shard_map/dot_general | solution.py:22
  251.0 1.0 fusion.21
  252.0 0.5 copy-done.3
  252.5 2.7 add_convert_fusion.1
  255.2 0.3 reduce-scatter.5.cloned.1.call-start
  255.5 1.0 fusion.2
  256.5 0.7 fusion.3
  257.2 1.7 fusion.4
  259.0 1.0 fusion.18
  260.0 1.0 add_convert_fusion
  261.0 0.3 pad_maximum_fusion
  261.3 55.3 %all_to_all.29 = bf16[32,24,2176]{2,1,0:T(8,128)(2,1)S(1)} all-to-all(bf16[32,24,2176]{2,1,0:T(8,128)(2,1)S(1)} %bitcast.90), channel_id=1, replica_groups=mesh['seq'=4,'zlo'=2,'y'=4,'x'=4,'core'=2] {'y','x','core'}, dimensions={0} | all-to-all | bytes 6684672 | tf_op jit(solution)/shard_map/all_to_all | solution.py:112
  316.6 5.7 %fusion.1 = bf16[1024,2176]{1,0:T(8,128)(2,1)} fusion(bf16[768,2176]{1,0:T(8,128)(2,1)S(1)} %bitcast.92, s32[1024]{0:T(1024)S(1)} %bitcast.99), kind=kOutput, calls=%fused_computation.11 | convolution fusion | flops 3423338496 | bytes 7802880 | tf_op jit(solution)/shard_map/dot_general | solution.py:18
  322.3 6.4 %reduce-scatter.3.cloned.1.call-done = bf16[192,2048]{1,0:T(8,128)(2,1)} async-done(((bf16[768,2048]{1,0:T(8,128)(2,1)}), bf16[192,2048]{1,0:T(8,128)(2,1)}) %reduce-scatter.3.cloned.1.call-update) | async-done | bytes 786448 | tf_op jit(solution)/shard_map/reduce_scatter | solution.py:105
  328.7 3.3 reshape.282
  332.0 8.1 %all-to-all-start.3 = ((bf16[64,3,2048]{2,1,0:T(4,128)(2,1)}), bf16[64,3,2048]{2,1,0:T(4,128)(2,1)S(1)}, u32[]{:S(2)}, u32[]{:S(2)}) async-start(bf16[64,3,2048]{2,1,0:T(4,128)(2,1)} %reshape.282), calls=%async_computation.4 | async-start | bytes 2097152 | tf_op jit(solution)/shard_map/all_to_all | solution.py:116
  340.1 5.8 %convolution_bitcast_fusion.2 = bf16[1,192,4096]{2,1,0:T(8,128)(2,1)} fusion(bf16[768,192]{0,1:T(8,128)(2,1)S(1)} %fusion.4, bf16[768,4096]{1,0:T(8,128)(2,1)} %bitcast.20), kind=kOutput, calls=%fused_computation.5 | convolution fusion | flops 1207959552 | bytes 8159232 | tf_op jit(solution)/shard_map/dot_general | solution.py:26
  345.9 5.5 %convolution_bitcast_fusion.1 = bf16[1,192,4096]{2,1,0:T(8,128)(2,1)} fusion(bf16[768,192]{0,1:T(8,128)(2,1)S(1)} %copy-done.6, bf16[768,4096]{1,0:T(8,128)(2,1)} %bitcast.20), kind=kOutput, calls=%fused_computation.4 | convolution fusion | flops 1207959552 | bytes 8159232 | tf_op jit(solution)/shard_map/dot_general | solution.py:26
  351.5 2.6 convolution_bitcast_fusion
  354.1 13.2 %all-to-all-done.3 = bf16[64,3,2048]{2,1,0:T(4,128)(2,1)S(1)} async-done(((bf16[64,3,2048]{2,1,0:T(4,128)(2,1)}), bf16[64,3,2048]{2,1,0:T(4,128)(2,1)S(1)}, u32[]{:S(2)}, u32[]{:S(2)}) %all-to-all-start.3) | async-done | bytes 786464 | tf_op jit(solution)/shard_map/all_to_all | solution.py:116
  367.4 0.7 reshape.283
  368.1 0.3 fusion.25
  368.4 28.3 %reduce-scatter.5.cloned.1.call-done = bf16[128,2176]{1,0:T(8,128)(2,1)} async-done(((bf16[1024,2176]{1,0:T(8,128)(2,1)}), bf16[128,2176]{1,0:T(8,128)(2,1)}) %reduce-scatter.5.cloned.1.call-update) | async-done | bytes 557072 | tf_op jit(solution)/shard_map/reduce_scatter | solution.py:114
  396.8 0.8 slice_convert_fusion
  397.5 0.6 copy.21
  398.1 1.1 slice.50
  399.2 1.1 pad_maximum_fusion.1
  (51 shorter events, 0.3 us)
Async XLA Ops:
  7.2 238.4 %copy-start = (bf16[1,192,4096]{2,1,0:T(8,128)(2,1)S(1)}, bf16[1,192,4096]{2,1,0:T(8,128)(2,1)}, u32[]{:S(2)}) copy-start(bf16[1,192,4096]{2,1,0:T(8,128)(2,1)} %param.12) | copy-start | bytes 4718596
  7.2 121.2 %all-gather.5.cloned.1.call-start = ((), (), s32[]{:S(2)}) async-start(), calls=%async_computation.8 | async-start | bytes 9437184 | tf_op jit(solution)/shard_map/all_gather | solution.py:59
  11.3 12.9 %copy-start.8 = (bf16[128,1]{0,1:T(2,128)(2,1)S(1)}, bf16[128,1]{0,1:T(2,128)(2,1)}, u32[]{:S(2)}) copy-start(bf16[128,1]{0,1:T(2,128)(2,1)} %param.9) | copy-start | bytes 772
  11.3 12.9 %copy-start.7 = (s32[128,1]{0,1:T(1,128)S(1)}, s32[128,1]{0,1:T(1,128)}, u32[]{:S(2)}) copy-start(s32[128,1]{0,1:T(1,128)} %param.8) | copy-start | bytes 1540
  13.6 66.5 %all-to-all-start.1 = ((bf16[64,3,4096]{2,1,0:T(4,128)(2,1)}), bf16[64,3,4096]{2,1,0:T(4,128)(2,1)}, u32[]{:S(2)}, u32[]{:S(2)}) async-start(bf16[64,3,4096]{2,1,0:T(4,128)(2,1)} %reshape.278), calls=%async_computation.1 | async-start | bytes 4194304 | tf_op jit(solution)/shard_map/all_to_all | solution.py:62
  24.2 221.4 %all-gather.3.cloned.1.call-start = ((), (), s32[]{:S(2)}) async-start(), calls=%async_computation.7 | async-start | bytes 7864320 | tf_op jit(solution)/shard_map/all_gather | solution.py:63
  24.3 54.6 %collective-permute-start.5 = (f32[2,128]{1,0:T(2,128)S(1)}, f32[2,128]{1,0:T(2,128)S(1)}, u32[]{:S(2)}, u32[]{:S(2)}) collective-permute-start(f32[2,128]{1,0:T(2,128)S(1)} %pad_maximum_fusion.2), channel_id=1, source_target_pairs={{0,192},{32,224},{64,0},{96,32},{128,64},{160,96},{192,128},{224,1... | collective-permute-start | bytes 3080 | tf_op jit(solution)/shard_map/ppermute | solution.py:32
  29.5 49.4 %collective-permute-start.4 = (f32[2,128]{1,0:T(2,128)S(1)}, f32[2,128]{1,0:T(2,128)S(1)}, u32[]{:S(2)}, u32[]{:S(2)}) collective-permute-start(f32[2,128]{1,0:T(2,128)S(1)} %pad_maximum_fusion.2), channel_id=1, source_target_pairs={{0,160},{32,192},{64,224},{96,0},{128,32},{160,64},{192,96},{224,1... | collective-permute-start | bytes 3080 | tf_op jit(solution)/shard_map/ppermute | solution.py:32
  30.9 47.9 %collective-permute-start.3 = (f32[2,128]{1,0:T(2,128)S(1)}, f32[2,128]{1,0:T(2,128)S(1)}, u32[]{:S(2)}, u32[]{:S(2)}) collective-permute-start(f32[2,128]{1,0:T(2,128)S(1)} %pad_maximum_fusion.2), channel_id=1, source_target_pairs={{0,128},{32,160},{64,192},{96,224},{128,0},{160,32},{192,64},{224,... | collective-permute-start | bytes 3080 | tf_op jit(solution)/shard_map/ppermute | solution.py:32
  35.2 43.7 %collective-permute-start.2 = (f32[2,128]{1,0:T(2,128)S(1)}, f32[2,128]{1,0:T(2,128)S(1)}, u32[]{:S(2)}, u32[]{:S(2)}) collective-permute-start(f32[2,128]{1,0:T(2,128)S(1)} %pad_maximum_fusion.2), channel_id=1, source_target_pairs={{0,96},{32,128},{64,160},{96,192},{128,224},{160,0},{192,32},{224,... | collective-permute-start | bytes 3080 | tf_op jit(solution)/shard_map/ppermute | solution.py:32
  35.2 32.9 %collective-permute-start = (f32[2,128]{1,0:T(2,128)S(1)}, f32[2,128]{1,0:T(2,128)S(1)}, u32[]{:S(2)}, u32[]{:S(2)}) collective-permute-start(f32[2,128]{1,0:T(2,128)S(1)} %pad_maximum_fusion.2), channel_id=1, source_target_pairs={{0,32},{32,64},{64,96},{96,128},{128,160},{160,192},{192,224},{224... | collective-permute-start | bytes 3080 | tf_op jit(solution)/shard_map/ppermute | solution.py:32
  68.0 7.2 %collective-permute-start.1 = (f32[2,128]{1,0:T(2,128)S(1)}, f32[2,128]{1,0:T(2,128)S(1)}, u32[]{:S(2)}, u32[]{:S(2)}) collective-permute-start(f32[2,128]{1,0:T(2,128)S(1)} %pad_maximum_fusion.2), channel_id=1, source_target_pairs={{0,64},{32,96},{64,128},{96,160},{128,192},{160,224},{192,0},{224,... | collective-permute-start | bytes 3080 | tf_op jit(solution)/shard_map/ppermute | solution.py:32
  75.3 4.3 %collective-permute-start.6 = (f32[2,128]{1,0:T(2,128)S(1)}, f32[2,128]{1,0:T(2,128)S(1)}, u32[]{:S(2)}, u32[]{:S(2)}) collective-permute-start(f32[2,128]{1,0:T(2,128)S(1)} %pad_maximum_fusion.2), channel_id=1, source_target_pairs={{0,224},{32,0},{64,32},{96,64},{128,96},{160,128},{192,160},{224,1... | collective-permute-start | bytes 3080 | tf_op jit(solution)/shard_map/ppermute | solution.py:32
  85.6 54.6 %all-to-all-start = ((f32[32,1,24]{2,1,0:T(1,128)}), f32[32,1,24]{2,1,0:T(1,128)S(1)}, u32[]{:S(2)}, u32[]{:S(2)}) async-start(f32[32,1,24]{2,1,0:T(1,128)} %bitcast.17), calls=%async_computation | async-start | bytes 32768 | tf_op jit(solution)/shard_map/all_to_all | solution.py:75
  140.2 80.6 %all-to-all-start.2 = ((bf16[32,24,4096]{2,1,0:T(8,128)(2,1)}), bf16[32,24,4096]{2,1,0:T(8,128)(2,1)}, u32[]{:S(2)}, u32[]{:S(2)}) async-start(bf16[32,24,4096]{2,1,0:T(8,128)(2,1)} %bitcast.91), calls=%async_computation.2 | async-start | bytes 12582912 | tf_op jit(solution)/shard_map/all_to_all | solution.py:78
  147.8 180.9 %reduce-scatter.3.cloned.1.call-start = ((), (), s32[]{:S(2)}) async-start(), calls=%async_computation.9 | async-start | bytes 3932160 | tf_op jit(solution)/shard_map/reduce_scatter | solution.py:105
  220.8 5.6 %copy-start.2 = (bf16[1,192,4096]{2,1,0:T(8,128)(2,1)S(1)}, bf16[1,192,4096]{2,1,0:T(8,128)(2,1)}, u32[]{:S(2)}) copy-start(bf16[1,192,4096]{2,1,0:T(8,128)(2,1)} %param.10) | copy-start | bytes 4718596
  251.0 1.1 copy-start.4
  251.0 1.5 copy-start.3
  255.2 141.5 %reduce-scatter.5.cloned.1.call-start = ((), (), s32[]{:S(2)}) async-start(), calls=%async_computation.10 | async-start | bytes 5013504 | tf_op jit(solution)/shard_map/reduce_scatter | solution.py:114
  257.2 2.8 copy-start.5
  332.0 35.4 %all-to-all-start.3 = ((bf16[64,3,2048]{2,1,0:T(4,128)(2,1)}), bf16[64,3,2048]{2,1,0:T(4,128)(2,1)S(1)}, u32[]{:S(2)}, u32[]{:S(2)}) async-start(bf16[64,3,2048]{2,1,0:T(4,128)(2,1)} %reshape.282), calls=%async_computation.4 | async-start | bytes 2097152 | tf_op jit(solution)/shard_map/all_to_all | solution.py:116
  340.1 5.9 %copy-start.6 = (bf16[768,192]{0,1:T(8,128)(2,1)S(1)}, bf16[768,192]{0,1:T(8,128)(2,1)}, u32[]{:S(2)}) copy-start(bf16[768,192]{0,1:T(8,128)(2,1)} %copy-done.5) | copy-start | bytes 884740
  340.1 11.4 %slice-start = ((s8[6291456]{0:T(1024)(128)(4,1)}), s8[4194304]{0:T(1024)(128)(4,1)S(1)}, s32[]{:S(2)}) async-start(s8[6291456]{0:T(1024)(128)(4,1)} %bitcast.102), calls=%async_computation.11 | async-start | bytes 8388608
  345.9 5.5 %slice-start.1 = ((s8[6291456]{0:T(1024)(128)(4,1)}), s8[2097152]{0:T(1024)(128)(4,1)S(1)}, s32[]{:S(2)}) async-start(s8[6291456]{0:T(1024)(128)(4,1)} %bitcast.102), calls=%async_computation.12 | async-start | bytes 4194304
  345.9 5.5 %copy-start.9 = (f32[768,384]{0,1:T(8,128)S(1)}, f32[768,384]{0,1:T(8,128)}, u32[]{:S(2)}) copy-start(f32[768,384]{0,1:T(8,128)} %fusion.5) | copy-start | bytes 3538948
  351.5 48.8 %copy-start.1 = (bf16[1,192,4096]{2,1,0:T(8,128)(2,1)S(1)}, bf16[1,192,4096]{2,1,0:T(8,128)(2,1)}, u32[]{:S(2)}) copy-start(bf16[1,192,4096]{2,1,0:T(8,128)(2,1)} %param.12) | copy-start | bytes 4718596
Sparse Core Ops, SparseCore 0:
  9.8 118.5 all-gather.4
  130.7 114.7 all-gather.2
  255.4 73.2 reduce-scatter.2
  331.1 65.5 reduce-scatter.4

commit v2 on v1

v2 whole, which is shorter than its diff:
```python
import jax
import jax.numpy as jnp
import numpy as np
from jax import lax
from jax.sharding import Mesh, PartitionSpec as P

CAP = 3
ZLO = 2
LANES = 128
COLUMN = ("seq", "zlo")
PLANE = ("y", "x", "core")
EXPERT = ("zlo", "y", "x", "core")
BF = jnp.bfloat16
F32 = jnp.float32


def dot(a, b, out=F32):
    return lax.dot_general(a, b, (((1,), (0,)), ((), ())), preferred_element_type=out)


def dot_t(a, b, out=F32):
    return lax.dot_general(a, b, (((1,), (1,)), ((), ())), preferred_element_type=out)


def tdot(a, b, out=F32):
    return lax.dot_general(a, b, (((0,), (0,)), ((), ())), preferred_element_type=out)


def shift(value, axis, count, by):
    return lax.ppermute(value, axis, [(i, (i + by) % count) for i in range(count)])


def ring_gather(parts, axis, count):
    got = [{0: parts[0]}, {0: parts[1]}]
    ahead, behind = list(parts), list(parts)
    for step in range(1, count // 2):
        for part in range(2):
            ahead[part] = shift(ahead[part], axis, count, 1)
            behind[part] = shift(behind[part], axis, count, -1)
            got[part][step] = ahead[part]
            got[part][count - step] = behind[part]
    got[0][count // 2] = shift(ahead[0], axis, count, 1)
    got[1][count // 2] = shift(behind[1], axis, count, -1)
    return got


def ring_scatter(block, axis, count):
    def total(value, carried):
        return value if carried is None else value + carried.astype(F32)

    far = count // 2
    ahead = [shift(block(far, 0).astype(BF), axis, count, 1), None]
    behind = [None, shift(block(far, 1).astype(BF), axis, count, -1)]
    for step in range(far - 1, 0, -1):
        for part in range(2):
            other = 1 - part
            ahead[other] = shift(total(block(count - step, other), ahead[other]).astype(BF), axis, count, 1)
            behind[part] = shift(total(block(step, part), behind[part]).astype(BF), axis, count, -1)
    return [total(total(block(0, part), ahead[part]), behind[part]) for part in range(2)]


def per_device(tokens, expert_ids, gate_weights, w_gate, w_up, w_down, cotangent):
    groups = lax.axis_size("seq")
    plane = lax.axis_size(PLANE)
    depth = groups * ZLO
    experts = plane * ZLO
    rows, width = tokens.shape
    half = width // 2
    send = experts * CAP
    held = send * groups
    block = depth * CAP
    zlo = lax.axis_index("zlo")
    group = lax.axis_index("seq")
    me = group * ZLO + zlo
    wg, wu, wd = w_gate[0], w_up[0], w_down[0]
    hidden = wg.shape[0]

    ids = expert_ids[:, 0]
    here = lax.iota(jnp.int32, rows)
    same = (ids[:, None] == ids[None, :]) & (here[None, :] < here[:, None])
    rank = jnp.sum(same.astype(jnp.int32), axis=1)
    slot = ids * CAP + rank
    from_slot = (slot[:, None] == lax.iota(jnp.int32, send)[None, :]).astype(BF)

    part_rows = rows // 2
    notes = jnp.stack(
        [slot[:part_rows].astype(BF), slot[part_rows:].astype(BF),
         gate_weights[:part_rows, 0], gate_weights[part_rows:, 0]], axis=1)
    notes = jnp.pad(notes, ((0, 0), (0, LANES - 4)))
    second = jnp.concatenate([tokens[part_rows:], notes], axis=1)
    x_got = ring_gather([tokens[:part_rows], second], COLUMN, depth)

    dy_send = tdot(from_slot, cotangent, BF).reshape(experts, CAP, width)
    dy_mine = lax.all_to_all(dy_send, EXPERT, 0, 0, tiled=True).reshape(send, width)
    dy_got = ring_gather([dy_mine[:send // 2], dy_mine[send // 2:]], "seq", groups)
    dy_held = jnp.concatenate([dy_got[part][d] for d in range(groups) for part in range(2)], axis=0)

    def places(d, part):
        noted = x_got[1][d][:, width:width + 4].astype(F32)
        slots = noted[:, part].astype(jnp.int32)
        of = slots // CAP
        row = (of % plane) * block + lax.rem(me - d + depth, depth) * CAP + slots % CAP
        return jnp.where(of // plane == zlo, row, -1), noted[:, 2 + part]

    order = [(d, part) for d in (*range(0, depth // 2 - 1), *range(depth // 2 + 2, depth)) for part in range(2)]
    late = [(d, part) for d in (depth // 2 - 1, depth // 2 + 1, depth // 2) for part in range(2)]
    at = lax.iota(jnp.int32, held)
    unpick, gate_send, x_send = {}, 0.0, []
    for keys in (order, late):
        noted = [places(*key) for key in keys]
        hits = jnp.concatenate([n[0] for n in noted])[:, None] == at[None, :]
        gates = jnp.concatenate([n[1] for n in noted])[:, None]
        gate_send = gate_send + jnp.sum(jnp.where(hits, gates, 0.0), axis=0)
        rows_in = jnp.concatenate([x_got[part][d][:, :width] for d, part in keys], axis=0)
        x_send.append(tdot(hits.astype(BF), rows_in))
        for key, n in zip(keys, noted):
            unpick[key] = n[0]
    x_send = (x_send[0].astype(BF).astype(F32) + x_send[1]).astype(BF)
    x_held = lax.all_to_all(x_send.reshape(plane, block, width), PLANE, 0, 0, tiled=True).reshape(held, width)
    gate_x = lax.all_to_all(gate_send.reshape(plane, block), PLANE, 0, 0, tiled=True).reshape(held)

    of_group = lax.rem(group - at // send + groups, groups)
    of_zlo = at % send // (plane * CAP)
    as_x = at % (plane * CAP) // CAP * block + (of_group * ZLO + of_zlo) * CAP + at % CAP
    turn = as_x[:, None] == at[None, :]
    turn_bf = turn.astype(BF)
    w_both = jnp.concatenate([wg, wu], axis=0)
    pre = lax.dot_general(
        turn.astype(F32), dot_t(x_held, w_both), (((1,), (0,)), ((), ())), precision=lax.Precision.HIGHEST,
        preferred_element_type=F32,
    )
    pre_gate, pre_up = pre[:, :hidden], pre[:, hidden:]
    gate_col = jnp.sum(jnp.where(turn, gate_x[None, :], 0.0), axis=1)[:, None]

    back = dot_t(dy_held, wd)
    sigmoid_gate = jax.nn.sigmoid(pre_gate)
    silu_gate = pre_gate * sigmoid_gate
    activated = silu_gate * pre_up
    route = jnp.sum(activated * back, axis=1, keepdims=True).astype(BF)
    scaled = (gate_col * activated).astype(BF)
    gated_back = gate_col * back
    g_gate = (gated_back * pre_up * sigmoid_gate * (1.0 + pre_gate * (1.0 - sigmoid_gate))).astype(BF)
    g_up = (gated_back * silu_gate).astype(BF)
    g_both = jnp.concatenate([g_gate, g_up], axis=1)

    w_a = w_both[:, :half]
    part_send = send // 2

    def block_a(d, part):
        first = d * send + part * part_send
        return dot(g_both[first:first + part_send], w_a)

    sum_a = jnp.concatenate([s.astype(BF) for s in ring_scatter(block_a, "seq", groups)], axis=0)

    g_x = tdot(turn_bf, jnp.concatenate([g_both, jnp.pad(route, ((0, 0), (0, LANES - 1)))], axis=1), BF)
    w_b = jnp.pad(w_both[:, half:], ((0, LANES), (0, LANES)))
    route_at = (lax.broadcasted_iota(jnp.int32, w_b.shape, 0) == 2 * hidden) & (
        lax.broadcasted_iota(jnp.int32, w_b.shape, 1) == half)
    w_b = jnp.where(route_at, jnp.ones((), BF), w_b)
    part_b = dot(g_x, w_b, BF)
    back_b = lax.all_to_all(part_b.reshape(plane, block, half + LANES), PLANE, 0, 0, tiled=True)
    back_b = back_b.reshape(held, half + LANES)

    def block_b(d, part):
        return dot((unpick[d, part][:, None] == at[None, :]).astype(BF), back_b)

    sum_b = jnp.concatenate(ring_scatter(block_b, COLUMN, depth), axis=0)

    back_a = lax.all_to_all(sum_a.reshape(experts, CAP, half), EXPERT, 0, 0, tiled=True)
    rows_a = dot(from_slot, back_a.reshape(send, half), BF)

    grad_gate = tdot(g_x[:, :hidden], x_held, BF)
    grad_up = tdot(g_x[:, hidden:2 * hidden], x_held, BF)
    grad_down = tdot(scaled, dy_held, BF)

    d_tokens = jnp.concatenate([rows_a, sum_b[:, :half].astype(BF)], axis=1)
    d_gates = sum_b[:, half:half + 1]
    return (d_tokens, d_gates, grad_gate[None], grad_up[None], grad_down[None])


def solution(mesh):
    groups, experts = mesh.shape["seq"], mesh.shape["expert"]
    side = int(np.sqrt(experts // (2 * ZLO)))
    fine = Mesh(
        np.asarray(mesh.devices).reshape(groups, ZLO, experts // (2 * ZLO * side), side, 2),
        ("seq", "zlo", "y", "x", "core"),
    )
    by_row = P(("seq",) + EXPERT, None)
    by_expert = P(EXPERT, "seq", None)
    return jax.shard_map(
        per_device,
        mesh=fine,
        in_specs=(by_row, by_row, by_row, by_expert, by_expert, by_expert, by_row),
        out_specs=(by_row, by_row, by_expert, by_expert, by_expert),
        check_vma=False,
    )
```

time: 408 us -> 487 us (1.19)
  the two profiles are of different devices: /device:TPU:1 before, /device:TPU:10 now
where the time goes in v2:
time: 487 us; the launch traced here: 477 us
  waiting for transfers between devices  223 us (46%)
  starting transfers between devices  111 us (23%)
  matrix products  73.6 us (15%)
  local copies, waits for them, and re-layouts  59.1 us (12%)
  other arithmetic  9.46 us (2%)
    ppermute x40, waiting for transfers between devices, shift(): lax.ppermute(value, axis, [(i, (i + by) % count) for i in range(count)])  178 us
    ppermute x40, starting transfers between devices, shift(): lax.ppermute(value, axis, [(i, (i + by) % count) for i in range(count)])  72.8 us
    dot_general x7, matrix products, tdot(): lax.dot_general(a, b, (((0,), (0,)), ((), ())), preferred_element_type=out)  37.5 us
    unnamed x57, local copies, waits for them, and re-layouts  32.2 us
    dot_general x26, matrix products, dot(): lax.dot_general(a, b, (((1,), (0,)), ((), ())), preferred_element_type=out)  22 us
    all_to_all x1, waiting for transfers between devices, per_device(): lax.all_to_all(part_b.reshape(plane, block, half + LANES), PLANE, 0, 0, t...  17.5 us
    all_to_all x1, waiting for transfers between devices, per_device(): lax.all_to_all(dy_send, EXPERT, 0, 0, tiled=True).reshape(send, width)  14.4 us
    dot_general x2, matrix products, dot_t(): lax.dot_general(a, b, (((1,), (1,)), ((), ())), preferred_element_type=out)  12.1 us
  transfers between devices with their start and end apart: 45, of which 23 were waited for; matrix products, arithmetic and copies ran while one was open for 24% of the time, Pallas kernels for 0%

profile of v2, /device:TPU:10, one launch (start us, length us, event | category | flops | bytes accessed | tf_op | source)
XLA Modules:
  0.0 477.2 jit_solution(407511769767765521)
XLA Ops:
  3.3 2.1 fusion.264
  6.3 1.9 collective-permute-start
  8.2 3.9 collective-permute-start.2
  12.1 3.2 collective-permute-start.15
  18.5 2.3 reshape.264
  20.8 15.2 %collective-permute-done.13 = bf16[64,4096]{1,0:T(8,128)(2,1)} collective-permute-done((bf16[64,4096]{1,0:T(8,128)(2,1)}, bf16[64,4096]{1,0:T(8,128)(2,1)}, u32[]{:S(2)}, u32[]{:S(2)}) %collective-permute-start.13) | collective-permute-done | bytes 524320 | tf_op jit(solution)/shard_map/ppermute | solution.py:30
  35.9 3.2 collective-permute-start.16
  41.1 3.2 collective-permute-start.3
  47.9 4.5 collective-permute-done.14
  52.3 3.2 collective-permute-start.18
  57.4 6.4 %collective-permute-done.1 = bf16[64,4224]{1,0:T(8,128)(2,1)S(1)} collective-permute-done((bf16[64,4224]{1,0:T(8,128)(2,1)}, bf16[64,4224]{1,0:T(8,128)(2,1)S(1)}, u32[]{:S(2)}, u32[]{:S(2)}) %collective-permute-start.1) | collective-permute-done | bytes 540704 | tf_op jit(solution)/shard_map/ppermute | solution.py:30
  64.2 3.2 collective-permute-start.5
  77.2 9.4 %collective-permute-done.4 = bf16[64,4224]{1,0:T(8,128)(2,1)S(1)} collective-permute-done((bf16[64,4224]{1,0:T(8,128)(2,1)S(1)}, bf16[64,4224]{1,0:T(8,128)(2,1)S(1)}, u32[]{:S(2)}, u32[]{:S(2)}) %collective-permute-start.4) | collective-permute-done | bytes 540704 | tf_op jit(solution)/shard_map/ppermute | solution.py:30
  87.7 9.8 %convolution_convert_fusion = bf16[768,4096]{1,0:T(8,128)(2,1)} fusion(bf16[640,4096]{1,0:T(8,128)(2,1)} %slice_dynamic-update-slice_fusion.3, s32[640]{0:T(1024)S(1)} %concatenate.45), kind=kOutput, calls=%fused_computation.1 | convolution fusion | flops 4030169088 | bytes 11536896 | tf_op jit(solution)/shard_map/dot_general | solution.py:26
  99.2 9.0 %collective-permute-done.6 = bf16[64,4224]{1,0:T(8,128)(2,1)S(1)} collective-permute-done((bf16[64,4224]{1,0:T(8,128)(2,1)S(1)}, bf16[64,4224]{1,0:T(8,128)(2,1)S(1)}, u32[]{:S(2)}, u32[]{:S(2)}) %collective-permute-start.6) | collective-permute-done | bytes 540704 | tf_op jit(solution)/shard_map/ppermute | solution.py:30
  109.5 7.5 %all-to-all-start = ((f32[32,1,24]{2,1,0:T(1,128)}), f32[32,1,24]{2,1,0:T(1,128)S(1)}, u32[]{:S(2)}, u32[]{:S(2)}) async-start(f32[32,1,24]{2,1,0:T(1,128)} %bitcast.69), calls=%async_computation | async-start | bytes 32768 | tf_op jit(solution)/shard_map/all_to_all | solution.py:120
  118.9 3.3 all-to-all-done
  122.2 7.3 %all-to-all-start.1 = ((bf16[64,3,4096]{2,1,0:T(4,128)(2,1)}), bf16[64,3,4096]{2,1,0:T(4,128)(2,1)}, u32[]{:S(2)}, u32[]{:S(2)}) async-start(bf16[64,3,4096]{2,1,0:T(4,128)(2,1)} %reshape.264), calls=%async_computation.1 | async-start | bytes 4194304 | tf_op jit(solution)/shard_map/all_to_all | solution.py:94
  133.1 8.4 %add_convert_fusion = bf16[768,4096]{1,0:T(8,128)(2,1)} fusion(bf16[768,4096]{1,0:T(8,128)(2,1)} %convolution_convert_fusion, bf16[384,4096]{1,0:T(8,128)(2,1)} %slice_dynamic-update-slice_fusion, s32[384]{0:T(512)S(1)} %concatenate.47), kind=kOutput, calls=%fused_computation | convolution fusion | flops 2425651200 | bytes 15730176 | tf_op jit(solution)/shard_map/dot_general | solution.py:26
  141.5 14.4 %all-to-all-done.1 = bf16[64,3,4096]{2,1,0:T(4,128)(2,1)} async-done(((bf16[64,3,4096]{2,1,0:T(4,128)(2,1)}), bf16[64,3,4096]{2,1,0:T(4,128)(2,1)}, u32[]{:S(2)}, u32[]{:S(2)}) %all-to-all-start.1) | async-done | bytes 1572896 | tf_op jit(solution)/shard_map/all_to_all | solution.py:94
  156.0 8.6 %all-to-all-start.2 = ((bf16[32,24,4096]{2,1,0:T(8,128)(2,1)}), bf16[32,24,4096]{2,1,0:T(8,128)(2,1)}, u32[]{:S(2)}, u32[]{:S(2)}) async-start(bf16[32,24,4096]{2,1,0:T(8,128)(2,1)} %bitcast.385), calls=%async_computation.2 | async-start | bytes 12582912 | tf_op jit(solution)/shard_map/all_to_all | solution.py:119
  164.6 2.9 fusion.7
  169.3 4.4 fusion.263
  173.7 2.5 slice.276
  177.3 3.0 collective-permute-start.10
  180.3 2.5 slice.274
  183.2 4.1 collective-permute-start.12
  187.3 2.1 constant_dynamic-update-slice_fusion.7
  189.4 2.1 constant_dynamic-update-slice_fusion.6
  191.5 55.5 %collective-permute-done.7 = bf16[96,4096]{1,0:T(8,128)(2,1)S(1)} collective-permute-done((bf16[96,4096]{1,0:T(8,128)(2,1)}, bf16[96,4096]{1,0:T(8,128)(2,1)S(1)}, u32[]{:S(2)}, u32[]{:S(2)}) %collective-permute-start.7) | collective-permute-done | bytes 786464 | tf_op jit(solution)/shard_map/ppermute | solution.py:30
  247.0 2.0 collective-permute-start.9
  249.0 2.1 collective-permute-start.11
  252.1 2.1 constant_dynamic-update-slice_fusion.4
  254.2 28.2 %collective-permute-done.9 = bf16[96,4096]{1,0:T(8,128)(2,1)S(1)} collective-permute-done((bf16[96,4096]{1,0:T(8,128)(2,1)S(1)}, bf16[96,4096]{1,0:T(8,128)(2,1)S(1)}, u32[]{:S(2)}, u32[]{:S(2)}) %collective-permute-start.9) | collective-permute-done | bytes 786464 | tf_op jit(solution)/shard_map/ppermute | solution.py:30
  285.3 2.1 constant_dynamic-update-slice_fusion
  287.3 6.5 %fusion = f32[768,384]{1,0:T(8,128)S(1)} fusion(bf16[768,4096]{1,0:T(8,128)(2,1)} %bitcast.72, bf16[192,4096]{1,0:T(8,128)(2,1)} %bitcast.388, bf16[192,4096]{1,0:T(8,128)(2,1)} %bitcast.390), kind=kOutput, calls=%fused_computation.15 | convolution fusion | flops 2422210560 | bytes 10616832 | tf_op jit(solution)/shard_map/dot_general | solution.py:22
  293.8 2.0 fusion.2
  295.8 5.6 %multiply_convert_fusion.2 = (bf16[768,192]{0,1:T(8,128)(2,1)S(1)}, bf16[768,192]{0,1:T(8,128)(2,1)S(1)}, bf16[768]{0:T(1024)(128)(2,1)S(1)}) fusion(f32[768,384]{0,1:T(8,128)S(1)} %fusion.2, f32[768]{0:T(1024)S(1)} %select_reduce_fusion, bf16[768,4096]{1,0:T(8,128)(2,1)} %constant_dynamic-update-slice_fusion, bf16[1,192,4096]{2,1,0:T(8,128)(2,1)S(1)} %copy-done), kind=kOutput, calls=%fused_computation.77 | convolution fusion | flops 1210465536 | bytes 9638400 | tf_op jit(solution)/shard_map/dot_general | solution.py:22
  302.9 2.0 collective-permute-start.20
  305.4 2.3 collective-permute-start.22
  309.1 18.9 %collective-permute-done.20 = bf16[96,2048]{1,0:T(8,128)(2,1)S(1)} collective-permute-done((bf16[96,2048]{1,0:T(8,128)(2,1)S(1)}, bf16[96,2048]{1,0:T(8,128)(2,1)S(1)}, u32[]{:S(2)}, u32[]{:S(2)}) %collective-permute-start.20) | collective-permute-done | bytes 393248 | tf_op jit(solution)/shard_map/ppermute | solution.py:30
  328.5 2.4 collective-permute-start.21
  332.6 3.7 collective-permute-start.25
  336.2 6.4 %collective-permute-done.21 = bf16[96,2048]{1,0:T(8,128)(2,1)S(1)} collective-permute-done((bf16[96,2048]{1,0:T(8,128)(2,1)S(1)}, bf16[96,2048]{1,0:T(8,128)(2,1)S(1)}, u32[]{:S(2)}, u32[]{:S(2)}) %collective-permute-start.21) | collective-permute-done | bytes 393248 | tf_op jit(solution)/shard_map/ppermute | solution.py:30
  342.8 7.3 %collective-permute-done.23 = bf16[96,2048]{1,0:T(8,128)(2,1)S(1)} collective-permute-done((bf16[96,2048]{1,0:T(8,128)(2,1)S(1)}, bf16[96,2048]{1,0:T(8,128)(2,1)S(1)}, u32[]{:S(2)}, u32[]{:S(2)}) %collective-permute-start.23) | collective-permute-done | bytes 393248 | tf_op jit(solution)/shard_map/ppermute | solution.py:30
  351.6 7.9 %all-to-all-start.3 = ((bf16[64,3,2048]{2,1,0:T(4,128)(2,1)}), bf16[64,3,2048]{2,1,0:T(4,128)(2,1)}, u32[]{:S(2)}, u32[]{:S(2)}) async-start(bf16[64,3,2048]{2,1,0:T(4,128)(2,1)} %reshape.267), calls=%async_computation.3 | async-start | bytes 2097152 | tf_op jit(solution)/shard_map/all_to_all | solution.py:169
  361.0 4.0 fusion.3
  364.9 9.9 %all-to-all-done.3 = bf16[64,3,2048]{2,1,0:T(4,128)(2,1)} async-done(((bf16[64,3,2048]{2,1,0:T(4,128)(2,1)}), bf16[64,3,2048]{2,1,0:T(4,128)(2,1)}, u32[]{:S(2)}, u32[]{:S(2)}) %all-to-all-start.3) | async-done | bytes 786464 | tf_op jit(solution)/shard_map/all_to_all | solution.py:169
  374.8 6.5 %all-to-all-start.4 = ((bf16[32,24,2176]{2,1,0:T(8,128)(2,1)}), bf16[32,24,2176]{2,1,0:T(8,128)(2,1)S(1)}, u32[]{:S(2)}, u32[]{:S(2)}) async-start(bf16[32,24,2176]{2,1,0:T(8,128)(2,1)} %bitcast.386), calls=%async_computation.4 | async-start | bytes 6684672 | tf_op jit(solution)/shard_map/all_to_all | solution.py:161
  381.6 5.5 %convolution_bitcast_fusion.1 = bf16[1,192,4096]{2,1,0:T(8,128)(2,1)} fusion(bf16[768,4096]{1,0:T(8,128)(2,1)} %bitcast.72, bf16[768,512]{0,1:T(8,128)(2,1)} %copy-done.12), kind=kOutput, calls=%fused_computation.3 | convolution fusion | flops 1207959552 | bytes 8159232 | tf_op jit(solution)/shard_map/dot_general | solution.py:26
  387.1 5.5 %convolution_bitcast_fusion.2 = bf16[1,192,4096]{2,1,0:T(8,128)(2,1)} fusion(bf16[768,4096]{1,0:T(8,128)(2,1)} %bitcast.72, bf16[768,512]{0,1:T(8,128)(2,1)S(1)} %copy-done.13), kind=kOutput, calls=%fused_computation.4 | convolution fusion | flops 1207959552 | bytes 8159232 | tf_op jit(solution)/shard_map/dot_general | solution.py:26
  392.6 5.4 %convolution_bitcast_fusion = bf16[1,192,4096]{2,1,0:T(8,128)(2,1)} fusion(bf16[768,4096]{1,0:T(8,128)(2,1)} %constant_dynamic-update-slice_fusion, f32[768]{0:T(1024)S(1)} %select_reduce_fusion, f32[768,384]{0,1:T(8,128)S(1)} %copy-done.11), kind=kOutput, calls=%fused_computation.2 | convolution fusion | flops 1208991744 | bytes 9047040 | tf_op jit(solution)/shard_map/dot_general | solution.py:26
  398.0 3.2 reshape.268
  401.2 2.3 fusion.45
  403.5 17.5 %all-to-all-done.4 = bf16[32,24,2176]{2,1,0:T(8,128)(2,1)S(1)} async-done(((bf16[32,24,2176]{2,1,0:T(8,128)(2,1)}), bf16[32,24,2176]{2,1,0:T(8,128)(2,1)S(1)}, u32[]{:S(2)}, u32[]{:S(2)}) %all-to-all-start.4) | async-done | bytes 3342368 | tf_op jit(solution)/shard_map/all_to_all | solution.py:161
  432.5 3.0 collective-permute-start.30
  438.5 3.3 collective-permute-start.37
  443.4 3.3 collective-permute-start.31
  448.9 3.8 collective-permute-start.38
  454.9 3.8 collective-permute-start.32
  458.6 2.1 collective-permute-done.38
  460.8 3.8 collective-permute-start.39
  465.8 6.0 %collective-permute-done.39 = bf16[64,2176]{1,0:T(8,128)(2,1)S(1)} collective-permute-done((bf16[64,2176]{1,0:T(8,128)(2,1)S(1)}, bf16[64,2176]{1,0:T(8,128)(2,1)S(1)}, u32[]{:S(2)}, u32[]{:S(2)}) %collective-permute-start.39) | collective-permute-done | bytes 278560 | tf_op jit(solution)/shard_map/ppermute | solution.py:30
  472.0 3.0 collective-permute-done.29
  (198 shorter events, 73.0 us)
Async XLA Ops:
  0.6 295.2 %copy-start = (bf16[1,192,4096]{2,1,0:T(8,128)(2,1)S(1)}, bf16[1,192,4096]{2,1,0:T(8,128)(2,1)}, u32[]{:S(2)}) copy-start(bf16[1,192,4096]{2,1,0:T(8,128)(2,1)} %param.12) | copy-start | bytes 4718596
  0.6 15.8 %copy-start.9 = (s32[128,1]{0,1:T(1,128)S(1)}, s32[128,1]{0,1:T(1,128)}, u32[]{:S(2)}) copy-start(s32[128,1]{0,1:T(1,128)} %param.8) | copy-start | bytes 1540
  0.7 14.7 %copy-start.4 = (bf16[128,4096]{1,0:T(8,128)(2,1)S(1)}, bf16[128,4096]{1,0:T(8,128)(2,1)}, u32[]{:S(2)}) copy-start(bf16[128,4096]{1,0:T(8,128)(2,1)} %param.7) | copy-start | bytes 3145732
  6.3 34.8 %collective-permute-start = (bf16[64,4224]{1,0:T(8,128)(2,1)}, bf16[64,4224]{1,0:T(8,128)(2,1)}, u32[]{:S(2)}, u32[]{:S(2)}) collective-permute-start(bf16[64,4224]{1,0:T(8,128)(2,1)} %fusion.28), channel_id=1, source_target_pairs={{0,32},{32,64},{64,96},{96,128},{128,160},{160,192},{192,224},{224... | collective-permute-start | bytes 1622024 | tf_op jit(solution)/shard_map/ppermute | solution.py:30
  8.2 32.9 %collective-permute-start.2 = (bf16[64,4224]{1,0:T(8,128)(2,1)}, bf16[64,4224]{1,0:T(8,128)(2,1)}, u32[]{:S(2)}, u32[]{:S(2)}) collective-permute-start(bf16[64,4224]{1,0:T(8,128)(2,1)} %fusion.28), channel_id=1, source_target_pairs={{0,224},{32,0},{64,32},{96,64},{128,96},{160,128},{192,160},{224,1... | collective-permute-start | bytes 1622024 | tf_op jit(solution)/shard_map/ppermute | solution.py:30
  12.1 23.8 %collective-permute-start.13 = (bf16[64,4096]{1,0:T(8,128)(2,1)}, bf16[64,4096]{1,0:T(8,128)(2,1)}, u32[]{:S(2)}, u32[]{:S(2)}) collective-permute-start(bf16[64,4096]{1,0:T(8,128)(2,1)} %get-tuple-element.35), channel_id=1, source_target_pairs={{0,32},{32,64},{64,96},{96,128},{128,160},{160,192},{192,224},{224... | collective-permute-start | bytes 1572872 | tf_op jit(solution)/shard_map/ppermute | solution.py:30
  12.1 23.8 %collective-permute-start.15 = (bf16[64,4096]{1,0:T(8,128)(2,1)}, bf16[64,4096]{1,0:T(8,128)(2,1)}, u32[]{:S(2)}, u32[]{:S(2)}) collective-permute-start(bf16[64,4096]{1,0:T(8,128)(2,1)} %get-tuple-element.35), channel_id=1, source_target_pairs={{0,224},{32,0},{64,32},{96,64},{128,96},{160,128},{192,160},{224,1... | collective-permute-start | bytes 1572872 | tf_op jit(solution)/shard_map/ppermute | solution.py:30
  35.9 16.4 %collective-permute-start.14 = (bf16[64,4096]{1,0:T(8,128)(2,1)}, bf16[64,4096]{1,0:T(8,128)(2,1)}, u32[]{:S(2)}, u32[]{:S(2)}) collective-permute-start(bf16[64,4096]{1,0:T(8,128)(2,1)} %collective-permute-done.13), channel_id=1, source_target_pairs={{0,32},{32,64},{64,96},{96,128},{128,160},{160,192},{192,224},{224... | collective-permute-start | bytes 1572872 | tf_op jit(solution)/shard_map/ppermute | solution.py:30
  35.9 16.4 %collective-permute-start.16 = (bf16[64,4096]{1,0:T(8,128)(2,1)}, bf16[64,4096]{1,0:T(8,128)(2,1)}, u32[]{:S(2)}, u32[]{:S(2)}) collective-permute-start(bf16[64,4096]{1,0:T(8,128)(2,1)} %collective-permute-done.15), channel_id=1, source_target_pairs={{0,224},{32,0},{64,32},{96,64},{128,96},{160,128},{192,160},{224,1... | collective-permute-start | bytes 1572872 | tf_op jit(solution)/shard_map/ppermute | solution.py:30
  41.1 22.7 %collective-permute-start.1 = (bf16[64,4224]{1,0:T(8,128)(2,1)}, bf16[64,4224]{1,0:T(8,128)(2,1)S(1)}, u32[]{:S(2)}, u32[]{:S(2)}) collective-permute-start(bf16[64,4224]{1,0:T(8,128)(2,1)} %collective-permute-done), channel_id=1, source_target_pairs={{0,32},{32,64},{64,96},{96,128},{128,160},{160,192},{192,224},{224... | collective-permute-start | bytes 1622024 | tf_op jit(solution)/shard_map/ppermute | solution.py:30
  41.1 22.8 %collective-permute-start.3 = (bf16[64,4224]{1,0:T(8,128)(2,1)}, bf16[64,4224]{1,0:T(8,128)(2,1)S(1)}, u32[]{:S(2)}, u32[]{:S(2)}) collective-permute-start(bf16[64,4224]{1,0:T(8,128)(2,1)} %collective-permute-done.2), channel_id=1, source_target_pairs={{0,224},{32,0},{64,32},{96,64},{128,96},{160,128},{192,160},{224,1... | collective-permute-start | bytes 1622024 | tf_op jit(solution)/shard_map/ppermute | solution.py:30
  52.3 22.8 %collective-permute-start.17 = (bf16[64,4096]{1,0:T(8,128)(2,1)}, bf16[64,4096]{1,0:T(8,128)(2,1)}, u32[]{:S(2)}, u32[]{:S(2)}) collective-permute-start(bf16[64,4096]{1,0:T(8,128)(2,1)} %collective-permute-done.14), channel_id=1, source_target_pairs={{0,32},{32,64},{64,96},{96,128},{128,160},{160,192},{192,224},{224... | collective-permute-start | bytes 1572872 | tf_op jit(solution)/shard_map/ppermute | solution.py:30
  52.3 64.7 %collective-permute-start.18 = (bf16[64,4096]{1,0:T(8,128)(2,1)}, bf16[64,4096]{1,0:T(8,128)(2,1)}, u32[]{:S(2)}, u32[]{:S(2)}) collective-permute-start(bf16[64,4096]{1,0:T(8,128)(2,1)} %collective-permute-done.16), channel_id=1, source_target_pairs={{0,224},{32,0},{64,32},{96,64},{128,96},{160,128},{192,160},{224,1... | collective-permute-start | bytes 1572872 | tf_op jit(solution)/shard_map/ppermute | solution.py:30
  64.1 22.5 %collective-permute-start.4 = (bf16[64,4224]{1,0:T(8,128)(2,1)S(1)}, bf16[64,4224]{1,0:T(8,128)(2,1)S(1)}, u32[]{:S(2)}, u32[]{:S(2)}) collective-permute-start(bf16[64,4224]{1,0:T(8,128)(2,1)S(1)} %collective-permute-done.1), channel_id=1, source_target_pairs={{0,32},{32,64},{64,96},{96,128},{128,160},{160,192},{192,224},{224... | collective-permute-start | bytes 1622024 | tf_op jit(solution)/shard_map/ppermute | solution.py:30
  64.2 33.3 %collective-permute-start.5 = (bf16[64,4224]{1,0:T(8,128)(2,1)S(1)}, bf16[64,4224]{1,0:T(8,128)(2,1)S(1)}, u32[]{:S(2)}, u32[]{:S(2)}) collective-permute-start(bf16[64,4224]{1,0:T(8,128)(2,1)S(1)} %collective-permute-done.3), channel_id=1, source_target_pairs={{0,224},{32,0},{64,32},{96,64},{128,96},{160,128},{192,160},{224,1... | collective-permute-start | bytes 1622024 | tf_op jit(solution)/shard_map/ppermute | solution.py:30
  75.1 55.2 %collective-permute-start.19 = (bf16[64,4096]{1,0:T(8,128)(2,1)}, bf16[64,4096]{1,0:T(8,128)(2,1)}, u32[]{:S(2)}, u32[]{:S(2)}) collective-permute-start(bf16[64,4096]{1,0:T(8,128)(2,1)} %collective-permute-done.17), channel_id=1, source_target_pairs={{0,32},{32,64},{64,96},{96,128},{128,160},{160,192},{192,224},{224... | collective-permute-start | bytes 1572872 | tf_op jit(solution)/shard_map/ppermute | solution.py:30
  86.6 0.8 copy-start.7
  87.7 10.3 %copy-start.8 = (bf16[64,4224]{1,0:T(8,128)(2,1)S(1)}, bf16[64,4224]{1,0:T(8,128)(2,1)}, u32[]{:S(2)}) copy-start(bf16[64,4224]{1,0:T(8,128)(2,1)} %copy-done.7) | copy-start | bytes 1622020
  97.5 10.8 %collective-permute-start.6 = (bf16[64,4224]{1,0:T(8,128)(2,1)S(1)}, bf16[64,4224]{1,0:T(8,128)(2,1)S(1)}, u32[]{:S(2)}, u32[]{:S(2)}) collective-permute-start(bf16[64,4224]{1,0:T(8,128)(2,1)S(1)} %collective-permute-done.5), channel_id=1, source_target_pairs={{0,224},{32,0},{64,32},{96,64},{128,96},{160,128},{192,160},{224,1... | collective-permute-start | bytes 1622024 | tf_op jit(solution)/shard_map/ppermute | solution.py:30
  109.5 12.7 %all-to-all-start = ((f32[32,1,24]{2,1,0:T(1,128)}), f32[32,1,24]{2,1,0:T(1,128)S(1)}, u32[]{:S(2)}, u32[]{:S(2)}) async-start(f32[32,1,24]{2,1,0:T(1,128)} %bitcast.69), calls=%async_computation | async-start | bytes 32768 | tf_op jit(solution)/shard_map/all_to_all | solution.py:120
  122.2 33.8 %all-to-all-start.1 = ((bf16[64,3,4096]{2,1,0:T(4,128)(2,1)}), bf16[64,3,4096]{2,1,0:T(4,128)(2,1)}, u32[]{:S(2)}, u32[]{:S(2)}) async-start(bf16[64,3,4096]{2,1,0:T(4,128)(2,1)} %reshape.264), calls=%async_computation.1 | async-start | bytes 4194304 | tf_op jit(solution)/shard_map/all_to_all | solution.py:94
  156.0 131.4 %all-to-all-start.2 = ((bf16[32,24,4096]{2,1,0:T(8,128)(2,1)}), bf16[32,24,4096]{2,1,0:T(8,128)(2,1)}, u32[]{:S(2)}, u32[]{:S(2)}) async-start(bf16[32,24,4096]{2,1,0:T(8,128)(2,1)} %bitcast.385), calls=%async_computation.2 | async-start | bytes 12582912 | tf_op jit(solution)/shard_map/all_to_all | solution.py:119
  176.2 75.9 %collective-permute-start.8 = (bf16[96,4096]{1,0:T(8,128)(2,1)}, bf16[96,4096]{1,0:T(8,128)(2,1)}, u32[]{:S(2)}, u32[]{:S(2)}) collective-permute-start(bf16[96,4096]{1,0:T(8,128)(2,1)} %slice.276), channel_id=1, source_target_pairs={{0,64},{64,128},{128,192},{192,0},{1,65},{65,129},{129,193},{193,1... | collective-permute-start | bytes 2359304 | tf_op jit(solution)/shard_map/ppermute | solution.py:30
  177.3 71.7 %collective-permute-start.10 = (bf16[96,4096]{1,0:T(8,128)(2,1)}, bf16[96,4096]{1,0:T(8,128)(2,1)}, u32[]{:S(2)}, u32[]{:S(2)}) collective-permute-start(bf16[96,4096]{1,0:T(8,128)(2,1)} %slice.276), channel_id=1, source_target_pairs={{0,192},{64,0},{128,64},{192,128},{1,193},{65,1},{129,65},{193,129... | collective-permute-start | bytes 2359304 | tf_op jit(solution)/shard_map/ppermute | solution.py:30
  182.8 64.2 %collective-permute-start.7 = (bf16[96,4096]{1,0:T(8,128)(2,1)}, bf16[96,4096]{1,0:T(8,128)(2,1)S(1)}, u32[]{:S(2)}, u32[]{:S(2)}) collective-permute-start(bf16[96,4096]{1,0:T(8,128)(2,1)} %slice.274), channel_id=1, source_target_pairs={{0,64},{64,128},{128,192},{192,0},{1,65},{65,129},{129,193},{193,1... | collective-permute-start | bytes 2359304 | tf_op jit(solution)/shard_map/ppermute | solution.py:30
  183.2 101.1 %collective-permute-start.12 = (bf16[96,4096]{1,0:T(8,128)(2,1)}, bf16[96,4096]{1,0:T(8,128)(2,1)S(1)}, u32[]{:S(2)}, u32[]{:S(2)}) collective-permute-start(bf16[96,4096]{1,0:T(8,128)(2,1)} %slice.274), channel_id=1, source_target_pairs={{0,192},{64,0},{128,64},{192,128},{1,193},{65,1},{129,65},{193,129... | collective-permute-start | bytes 2359304 | tf_op jit(solution)/shard_map/ppermute | solution.py:30
  247.0 35.4 %collective-permute-start.9 = (bf16[96,4096]{1,0:T(8,128)(2,1)S(1)}, bf16[96,4096]{1,0:T(8,128)(2,1)S(1)}, u32[]{:S(2)}, u32[]{:S(2)}) collective-permute-start(bf16[96,4096]{1,0:T(8,128)(2,1)S(1)} %collective-permute-done.7), channel_id=1, source_target_pairs={{0,64},{64,128},{128,192},{192,0},{1,65},{65,129},{129,193},{193,1... | collective-permute-start | bytes 2359304 | tf_op jit(solution)/shard_map/ppermute | solution.py:30
  249.0 34.4 %collective-permute-start.11 = (bf16[96,4096]{1,0:T(8,128)(2,1)}, bf16[96,4096]{1,0:T(8,128)(2,1)S(1)}, u32[]{:S(2)}, u32[]{:S(2)}) collective-permute-start(bf16[96,4096]{1,0:T(8,128)(2,1)} %collective-permute-done.10), channel_id=1, source_target_pairs={{0,192},{64,0},{128,64},{192,128},{1,193},{65,1},{129,65},{193,129... | collective-permute-start | bytes 2359304 | tf_op jit(solution)/shard_map/ppermute | solution.py:30
  295.8 5.7 %copy-start.10 = (f32[768,384]{0,1:T(8,128)}, f32[768,384]{0,1:T(8,128)S(1)}, u32[]{:S(2)}) copy-start(f32[768,384]{0,1:T(8,128)S(1)} %fusion.2) | copy-start | bytes 3538948
  301.5 30.6 %copy-start.2 = (bf16[768,192]{0,1:T(8,128)(2,1)}, bf16[768,192]{0,1:T(8,128)(2,1)S(1)}, u32[]{:S(2)}) copy-start(bf16[768,192]{0,1:T(8,128)(2,1)S(1)} %get-tuple-element.32) | copy-start | bytes 884740
  302.9 25.1 %collective-permute-start.20 = (bf16[96,2048]{1,0:T(8,128)(2,1)S(1)}, bf16[96,2048]{1,0:T(8,128)(2,1)S(1)}, u32[]{:S(2)}, u32[]{:S(2)}) collective-permute-start(bf16[96,2048]{1,0:T(8,128)(2,1)S(1)} %convolution_convert_fusion.8), channel_id=1, source_target_pairs={{0,64},{64,128},{128,192},{192,0},{1,65},{65,129},{129,193},{193,1... | collective-permute-start | bytes 1179656 | tf_op jit(solution)/shard_map/ppermute | solution.py:30
  305.4 30.8 %collective-permute-start.22 = (bf16[96,2048]{1,0:T(8,128)(2,1)S(1)}, bf16[96,2048]{1,0:T(8,128)(2,1)S(1)}, u32[]{:S(2)}, u32[]{:S(2)}) collective-permute-start(bf16[96,2048]{1,0:T(8,128)(2,1)S(1)} %convolution_convert_fusion.7), channel_id=1, source_target_pairs={{0,192},{64,0},{128,64},{192,128},{1,193},{65,1},{129,65},{193,129... | collective-permute-start | bytes 1179656 | tf_op jit(solution)/shard_map/ppermute | solution.py:30
  307.7 24.3 %collective-permute-start.24 = (bf16[96,2048]{1,0:T(8,128)(2,1)S(1)}, bf16[96,2048]{1,0:T(8,128)(2,1)S(1)}, u32[]{:S(2)}, u32[]{:S(2)}) collective-permute-start(bf16[96,2048]{1,0:T(8,128)(2,1)S(1)} %convolution_convert_fusion.5), channel_id=1, source_target_pairs={{0,192},{64,0},{128,64},{192,128},{1,193},{65,1},{129,65},{193,129... | collective-permute-start | bytes 1179656 | tf_op jit(solution)/shard_map/ppermute | solution.py:30
  328.5 14.2 %collective-permute-start.21 = (bf16[96,2048]{1,0:T(8,128)(2,1)S(1)}, bf16[96,2048]{1,0:T(8,128)(2,1)S(1)}, u32[]{:S(2)}, u32[]{:S(2)}) collective-permute-start(bf16[96,2048]{1,0:T(8,128)(2,1)S(1)} %add_convert_fusion.4), channel_id=1, source_target_pairs={{0,64},{64,128},{128,192},{192,0},{1,65},{65,129},{129,193},{193,1... | collective-permute-start | bytes 1179656 | tf_op jit(solution)/shard_map/ppermute | solution.py:30
  331.4 18.7 %collective-permute-start.23 = (bf16[96,2048]{1,0:T(8,128)(2,1)S(1)}, bf16[96,2048]{1,0:T(8,128)(2,1)S(1)}, u32[]{:S(2)}, u32[]{:S(2)}) collective-permute-start(bf16[96,2048]{1,0:T(8,128)(2,1)S(1)} %convolution_convert_fusion.6), channel_id=1, source_target_pairs={{0,64},{64,128},{128,192},{192,0},{1,65},{65,129},{129,193},{193,1... | collective-permute-start | bytes 1179656 | tf_op jit(solution)/shard_map/ppermute | solution.py:30
  332.6 17.5 %collective-permute-start.25 = (bf16[96,2048]{1,0:T(8,128)(2,1)S(1)}, bf16[96,2048]{1,0:T(8,128)(2,1)S(1)}, u32[]{:S(2)}, u32[]{:S(2)}) collective-permute-start(bf16[96,2048]{1,0:T(8,128)(2,1)S(1)} %add_convert_fusion.2), channel_id=1, source_target_pairs={{0,192},{64,0},{128,64},{192,128},{1,193},{65,1},{129,65},{193,129... | collective-permute-start | bytes 1179656 | tf_op jit(solution)/shard_map/ppermute | solution.py:30
  350.2 9.4 %copy-start.3 = (bf16[768,192]{0,1:T(8,128)(2,1)S(1)}, bf16[768,192]{0,1:T(8,128)(2,1)}, u32[]{:S(2)}) copy-start(bf16[768,192]{0,1:T(8,128)(2,1)} %copy-done.2) | copy-start | bytes 884740
  351.6 23.2 %all-to-all-start.3 = ((bf16[64,3,2048]{2,1,0:T(4,128)(2,1)}), bf16[64,3,2048]{2,1,0:T(4,128)(2,1)}, u32[]{:S(2)}, u32[]{:S(2)}) async-start(bf16[64,3,2048]{2,1,0:T(4,128)(2,1)} %reshape.267), calls=%async_computation.3 | async-start | bytes 2097152 | tf_op jit(solution)/shard_map/all_to_all | solution.py:169
  359.6 1.4 copy-start.6
  360.6 4.4 copy-start.12
  374.8 46.2 %all-to-all-start.4 = ((bf16[32,24,2176]{2,1,0:T(8,128)(2,1)}), bf16[32,24,2176]{2,1,0:T(8,128)(2,1)S(1)}, u32[]{:S(2)}, u32[]{:S(2)}) async-start(bf16[32,24,2176]{2,1,0:T(8,128)(2,1)} %bitcast.386), calls=%async_computation.4 | async-start | bytes 6684672 | tf_op jit(solution)/shard_map/all_to_all | solution.py:161
  381.6 5.5 %copy-start.13 = (bf16[768,512]{0,1:T(8,128)(2,1)S(1)}, bf16[768,512]{0,1:T(8,128)(2,1)}, u32[]{:S(2)}) copy-start(bf16[768,512]{0,1:T(8,128)(2,1)} %copy-done.12) | copy-start | bytes 2359300
  387.1 5.5 %copy-start.11 = (f32[768,384]{0,1:T(8,128)S(1)}, f32[768,384]{0,1:T(8,128)}, u32[]{:S(2)}) copy-start(f32[768,384]{0,1:T(8,128)} %copy-done.10) | copy-start | bytes 3538948
  421.7 15.2 %collective-permute-start.33 = (bf16[64,2176]{1,0:T(8,128)(2,1)S(1)}, bf16[64,2176]{1,0:T(8,128)(2,1)S(1)}, u32[]{:S(2)}, u32[]{:S(2)}) collective-permute-start(bf16[64,2176]{1,0:T(8,128)(2,1)S(1)} %convolution_convert_fusion.2), channel_id=1, source_target_pairs={{0,32},{32,64},{64,96},{96,128},{128,160},{160,192},{192,224},{224... | collective-permute-start | bytes 835592 | tf_op jit(solution)/shard_map/ppermute | solution.py:30
  425.1 12.7 %collective-permute-start.36 = (bf16[64,2176]{1,0:T(8,128)(2,1)S(1)}, bf16[64,2176]{1,0:T(8,128)(2,1)S(1)}, u32[]{:S(2)}, u32[]{:S(2)}) collective-permute-start(bf16[64,2176]{1,0:T(8,128)(2,1)S(1)} %convolution_convert_fusion.1), channel_id=1, source_target_pairs={{0,224},{32,0},{64,32},{96,64},{128,96},{160,128},{192,160},{224,1... | collective-permute-start | bytes 835592 | tf_op jit(solution)/shard_map/ppermute | solution.py:30
  429.6 12.2 %collective-permute-start.26 = (bf16[64,2176]{1,0:T(8,128)(2,1)S(1)}, bf16[64,2176]{1,0:T(8,128)(2,1)S(1)}, u32[]{:S(2)}, u32[]{:S(2)}) collective-permute-start(bf16[64,2176]{1,0:T(8,128)(2,1)S(1)} %convolution_convert_fusion.4), channel_id=1, source_target_pairs={{0,32},{32,64},{64,96},{96,128},{128,160},{160,192},{192,224},{224... | collective-permute-start | bytes 835592 | tf_op jit(solution)/shard_map/ppermute | solution.py:30
  432.5 10.2 %collective-permute-start.30 = (bf16[64,2176]{1,0:T(8,128)(2,1)S(1)}, bf16[64,2176]{1,0:T(8,128)(2,1)S(1)}, u32[]{:S(2)}, u32[]{:S(2)}) collective-permute-start(bf16[64,2176]{1,0:T(8,128)(2,1)S(1)} %convolution_convert_fusion.3), channel_id=1, source_target_pairs={{0,224},{32,0},{64,32},{96,64},{128,96},{160,128},{192,160},{224,1... | collective-permute-start | bytes 835592 | tf_op jit(solution)/shard_map/ppermute | solution.py:30
  437.7 10.8 %collective-permute-start.34 = (bf16[64,2176]{1,0:T(8,128)(2,1)S(1)}, bf16[64,2176]{1,0:T(8,128)(2,1)S(1)}, u32[]{:S(2)}, u32[]{:S(2)}) collective-permute-start(bf16[64,2176]{1,0:T(8,128)(2,1)S(1)} %add_convert_fusion.9), channel_id=1, source_target_pairs={{0,32},{32,64},{64,96},{96,128},{128,160},{160,192},{192,224},{224... | collective-permute-start | bytes 835592 | tf_op jit(solution)/shard_map/ppermute | solution.py:30
  438.5 10.3 %collective-permute-start.37 = (bf16[64,2176]{1,0:T(8,128)(2,1)S(1)}, bf16[64,2176]{1,0:T(8,128)(2,1)S(1)}, u32[]{:S(2)}, u32[]{:S(2)}) collective-permute-start(bf16[64,2176]{1,0:T(8,128)(2,1)S(1)} %add_convert_fusion.7), channel_id=1, source_target_pairs={{0,224},{32,0},{64,32},{96,64},{128,96},{160,128},{192,160},{224,1... | collective-permute-start | bytes 835592 | tf_op jit(solution)/shard_map/ppermute | solution.py:30
  442.5 11.9 %collective-permute-start.27 = (bf16[64,2176]{1,0:T(8,128)(2,1)S(1)}, bf16[64,2176]{1,0:T(8,128)(2,1)S(1)}, u32[]{:S(2)}, u32[]{:S(2)}) collective-permute-start(bf16[64,2176]{1,0:T(8,128)(2,1)S(1)} %add_convert_fusion.14), channel_id=1, source_target_pairs={{0,32},{32,64},{64,96},{96,128},{128,160},{160,192},{192,224},{224... | collective-permute-start | bytes 835592 | tf_op jit(solution)/shard_map/ppermute | solution.py:30
  443.4 11.4 %collective-permute-start.31 = (bf16[64,2176]{1,0:T(8,128)(2,1)S(1)}, bf16[64,2176]{1,0:T(8,128)(2,1)S(1)}, u32[]{:S(2)}, u32[]{:S(2)}) collective-permute-start(bf16[64,2176]{1,0:T(8,128)(2,1)S(1)} %add_convert_fusion.11), channel_id=1, source_target_pairs={{0,224},{32,0},{64,32},{96,64},{128,96},{160,128},{192,160},{224,1... | collective-permute-start | bytes 835592 | tf_op jit(solution)/shard_map/ppermute | solution.py:30
  448.5 17.3 %collective-permute-start.35 = (bf16[64,2176]{1,0:T(8,128)(2,1)S(1)}, bf16[64,2176]{1,0:T(8,128)(2,1)S(1)}, u32[]{:S(2)}, u32[]{:S(2)}) collective-permute-start(bf16[64,2176]{1,0:T(8,128)(2,1)S(1)} %add_convert_fusion.8), channel_id=1, source_target_pairs={{0,32},{32,64},{64,96},{96,128},{128,160},{160,192},{192,224},{224... | collective-permute-start | bytes 835592 | tf_op jit(solution)/shard_map/ppermute | solution.py:30
  448.9 11.9 %collective-permute-start.38 = (bf16[64,2176]{1,0:T(8,128)(2,1)S(1)}, bf16[64,2176]{1,0:T(8,128)(2,1)S(1)}, u32[]{:S(2)}, u32[]{:S(2)}) collective-permute-start(bf16[64,2176]{1,0:T(8,128)(2,1)S(1)} %add_convert_fusion.6), channel_id=1, source_target_pairs={{0,224},{32,0},{64,32},{96,64},{128,96},{160,128},{192,160},{224,1... | collective-permute-start | bytes 835592 | tf_op jit(solution)/shard_map/ppermute | solution.py:30
  454.5 11.2 %collective-permute-start.28 = (bf16[64,2176]{1,0:T(8,128)(2,1)S(1)}, bf16[64,2176]{1,0:T(8,128)(2,1)S(1)}, u32[]{:S(2)}, u32[]{:S(2)}) collective-permute-start(bf16[64,2176]{1,0:T(8,128)(2,1)S(1)} %add_convert_fusion.13), channel_id=1, source_target_pairs={{0,32},{32,64},{64,96},{96,128},{128,160},{160,192},{192,224},{224... | collective-permute-start | bytes 835592 | tf_op jit(solution)/shard_map/ppermute | solution.py:30
  454.9 17.1 %collective-permute-start.32 = (bf16[64,2176]{1,0:T(8,128)(2,1)S(1)}, bf16[64,2176]{1,0:T(8,128)(2,1)S(1)}, u32[]{:S(2)}, u32[]{:S(2)}) collective-permute-start(bf16[64,2176]{1,0:T(8,128)(2,1)S(1)} %add_convert_fusion.10), channel_id=1, source_target_pairs={{0,224},{32,0},{64,32},{96,64},{128,96},{160,128},{192,160},{224,1... | collective-permute-start | bytes 835592 | tf_op jit(solution)/shard_map/ppermute | solution.py:30
  460.8 11.0 %collective-permute-start.39 = (bf16[64,2176]{1,0:T(8,128)(2,1)S(1)}, bf16[64,2176]{1,0:T(8,128)(2,1)S(1)}, u32[]{:S(2)}, u32[]{:S(2)}) collective-permute-start(bf16[64,2176]{1,0:T(8,128)(2,1)S(1)} %add_convert_fusion.5), channel_id=1, source_target_pairs={{0,224},{32,0},{64,32},{96,64},{128,96},{160,128},{192,160},{224,1... | collective-permute-start | bytes 835592 | tf_op jit(solution)/shard_map/ppermute | solution.py:30
  465.7 10.0 %copy-start.5 = (bf16[128,2048]{1,0:T(8,128)(2,1)S(1)}, bf16[128,2048]{1,0:T(8,128)(2,1)}, u32[]{:S(2)}) copy-start(bf16[128,2048]{1,0:T(8,128)(2,1)} %fusion.45) | copy-start | bytes 1572868
  465.7 9.3 %collective-permute-start.29 = (bf16[64,2176]{1,0:T(8,128)(2,1)S(1)}, bf16[64,2176]{1,0:T(8,128)(2,1)S(1)}, u32[]{:S(2)}, u32[]{:S(2)}) collective-permute-start(bf16[64,2176]{1,0:T(8,128)(2,1)S(1)} %add_convert_fusion.12), channel_id=1, source_target_pairs={{0,32},{32,64},{64,96},{96,128},{128,160},{160,192},{192,224},{224... | collective-permute-start | bytes 835592 | tf_op jit(solution)/shard_map/ppermute | solution.py:30
  471.9 4.9 %copy-start.1 = (bf16[1,192,4096]{2,1,0:T(8,128)(2,1)S(1)}, bf16[1,192,4096]{2,1,0:T(8,128)(2,1)}, u32[]{:S(2)}) copy-start(bf16[1,192,4096]{2,1,0:T(8,128)(2,1)} %param.12) | copy-start | bytes 4718596

commit v3 on v1

--- a/solution.py
+++ b/solution.py
@@ -26,14 +26,6 @@
     return lax.dot_general(a, b, (((0,), (0,)), ((), ())), preferred_element_type=out)
 
 
-def column_gather(values, depth, me):
-    got = [values]
-    for far in range(1, depth):
-        got.append(lax.ppermute(values, COLUMN, [(i, (i + far) % depth) for i in range(depth)]))
-    picked = lax.rem(me - lax.iota(jnp.int32, depth) + depth, depth)
-    return jnp.take(jnp.stack(got), picked, axis=0)
-
-
 def per_device(tokens, expert_ids, gate_weights, w_gate, w_up, w_down, cotangent):
     groups = lax.axis_size("seq")
     plane = lax.axis_size(PLANE)
@@ -45,7 +37,6 @@
     held = send * groups
     block = depth * CAP
     zlo = lax.axis_index("zlo")
-    me = lax.axis_index("seq") * ZLO + zlo
     wg, wu, wd = w_gate[0], w_up[0], w_down[0]
 
     ids = expert_ids[:, 0]
@@ -56,37 +47,42 @@
     to_slot = (slot[None, :] == lax.iota(jnp.int32, send)[:, None]).astype(BF)
     from_slot = (slot[:, None] == lax.iota(jnp.int32, send)[None, :]).astype(BF)
 
-    x_column = lax.all_gather(tokens, COLUMN, axis=0, tiled=True)
-
+    notes = jnp.pad(jnp.stack([slot.astype(BF), gate_weights[:, 0]], axis=1), ((0, 0), (0, LANES - 2)))
+    x_column = lax.all_gather(jnp.concatenate([tokens, notes], axis=1), COLUMN, axis=0, tiled=True)
     dy_send = dot(to_slot, cotangent, BF).reshape(experts, CAP, width)
     dy_mine = lax.all_to_all(dy_send, EXPERT, 0, 0, tiled=True).reshape(send, width)
+
+    slots = x_column[:, width].astype(jnp.int32)
+    to = slots // CAP
+    source = lax.iota(jnp.int32, depth * rows) // rows
+    target = jnp.where(to // plane == zlo, to % plane * block + source * CAP + slots % CAP, -1)
+    pick = (target[None, :] == lax.iota(jnp.int32, held)[:, None]).astype(BF)
+    unpick = (target[:, None] == lax.iota(jnp.int32, held)[None, :]).astype(BF)
+
+    def choose(column):
+        return dot(pick, column, BF).reshape(plane, block, column.shape[1])
+
+    def to_expert(chosen):
+        return lax.all_to_all(chosen, PLANE, 0, 0, tiled=True).reshape(held, chosen.shape[2])
+
     dy_held = lax.all_gather(dy_mine, "seq", axis=0, tiled=True)
-
-    code = (ids % plane) * block + me * CAP + rank + held * (ids // plane)
-    meta = jnp.stack([code.astype(F32), gate_weights[:, 0].astype(F32)])
-    meta = column_gather(meta, depth, me)
-    target = meta[:, 0, :].reshape(-1).astype(jnp.int32) - held * zlo
-    gates_column = meta[:, 1, :].reshape(-1)
-    in_column = depth * rows
-    hit = target[None, :] == lax.iota(jnp.int32, held)[:, None]
-    pick = hit.astype(BF)
-    unpick = (target[:, None] == lax.iota(jnp.int32, held)[None, :]).astype(BF)
-    gate_send = jnp.sum(jnp.where(hit, gates_column[None, :], 0.0), axis=1).reshape(plane, block)
-    gate_x = lax.all_to_all(gate_send, PLANE, 0, 0, tiled=True).reshape(held)
-
-    x_send = dot(pick, x_column, BF).reshape(plane, block, width)
-    x_held = lax.all_to_all(x_send, PLANE, 0, 0, tiled=True).reshape(held, width)
+    x_held = to_expert(choose(x_column))
+    gate_x = x_held[:, width + 1].astype(F32)
+    x_held = x_held[:, :width]
 
     at = lax.iota(jnp.int32, held)
     as_x = (at % (plane * CAP)) // CAP * block + at // (plane * CAP) * CAP + at % CAP
     turn = as_x[:, None] == at[None, :]
     turn_bf = turn.astype(BF)
     turn_f32 = turn.astype(F32)
-    pre_x = jnp.concatenate([dot_t(x_held, wg), dot_t(x_held, wu)], axis=1)
-    pre = lax.dot_general(
-        turn_f32, pre_x, (((1,), (0,)), ((), ())), precision=lax.Precision.HIGHEST,
-        preferred_element_type=F32,
-    )
+
+    def turned(value):
+        return lax.dot_general(
+            turn_f32, value, (((1,), (0,)), ((), ())), precision=lax.Precision.HIGHEST, preferred_element_type=F32,
+        )
+
+    w_both = jnp.concatenate([wg, wu], axis=0)
+    pre = turned(dot_t(x_held, w_both))
     hidden = wg.shape[0]
     pre_gate, pre_up = pre[:, :hidden], pre[:, hidden:]
     gate_col = jnp.sum(jnp.where(turn, gate_x[None, :], 0.0), axis=1)[:, None]

time: 408 us -> 412 us (level)
  waiting for transfers between devices: 199 us -> 230 us
  starting transfers between devices: 56.3 us -> 26.6 us
  other arithmetic: 5.4 us -> 12 us
    all_to_all x1, waiting for transfers between devices: 0.01 us -> 49 us  [per_device(): lax.all_to_all(dy_send, EXPERT, 0, 0, tiled=True).reshape(send, width)]
    ppermute x7 -> x0, waiting for transfers between devices: 34.9 us -> none  [column_gather(): lax.ppermute(values, COLUMN, [(i, (i + far) % depth) for i in range(depth)])]
    ppermute x7 -> x0, starting transfers between devices: 20.2 us -> none  [column_gather(): lax.ppermute(values, COLUMN, [(i, (i + far) % depth) for i in range(depth)])]
    all_gather x1, waiting for transfers between devices: 33.2 us -> 53.1 us  [per_device(): lax.all_gather(jnp.concatenate([tokens, notes], axis=1), COLUMN, axis=0,...]
    all_to_all x2 -> x1, starting transfers between devices: 17.1 us -> 7.58 us  [to_expert(): lax.all_to_all(chosen, PLANE, 0, 0, tiled=True)]
    dot_general x3 -> x2, matrix products: 16 us -> 11.4 us  [dot_t(): lax.dot_general(a, b, (((1,), (1,)), ((), ())), preferred_element_type=out)]
    all_gather x1, waiting for transfers between devices: 11.2 us -> 6.95 us  [per_device(): dy_held = lax.all_gather(dy_mine, 'seq', axis=0, tiled=True)]
    all_to_all x2 -> x1, waiting for transfers between devices: 71.1 us -> 75.4 us  [to_expert(): lax.all_to_all(chosen, PLANE, 0, 0, tiled=True)]
  transfers between devices with their start and end apart: 15 -> 7, of which waited for: 9 -> 7; matrix products, arithmetic and copies ran while one was open for 17% -> 16% of each run, Pallas kernels for 0% -> 0%
where the time goes in v3:
time: 412 us; the launch traced here: 411 us
  waiting for transfers between devices  230 us (56%)
  matrix products  60.5 us (15%)
  blocking collectives  54.8 us (13%)
  starting transfers between devices  26.6 us (6%)
  between operations  14 us (3%)
  local copies, waits for them, and re-layouts  12.9 us (3%)
  other arithmetic  12 us (3%)
    all_to_all x1, waiting for transfers between devices, to_expert(): lax.all_to_all(chosen, PLANE, 0, 0, tiled=True)  75.4 us
    all_to_all x1, blocking collectives, per_device(): lax.all_to_all(part_b.reshape(plane, block, half + LANES), PLANE, 0, 0, t...  54.8 us
    all_gather x1, waiting for transfers between devices, per_device(): lax.all_gather(jnp.concatenate([tokens, notes], axis=1), COLUMN, axis=0,...  53.1 us
    all_to_all x1, waiting for transfers between devices, per_device(): lax.all_to_all(dy_send, EXPERT, 0, 0, tiled=True).reshape(send, width)  49 us
    reduce_scatter x1, waiting for transfers between devices, per_device(): sum_b = lax.psum_scatter(column_b, COLUMN, scatter_dimension=0, tiled=True)  28.3 us
    dot_general x8, matrix products, dot(): lax.dot_general(a, b, (((1,), (0,)), ((), ())), preferred_element_type=out)  25.9 us
    dot_general x6, matrix products, tdot(): lax.dot_general(a, b, (((0,), (0,)), ((), ())), preferred_element_type=out)  20.2 us
    dot_general x2, matrix products, dot_t(): lax.dot_general(a, b, (((1,), (1,)), ((), ())), preferred_element_type=out)  11.4 us
  transfers between devices with their start and end apart: 7, of which 7 were waited for; matrix products, arithmetic and copies ran while one was open for 16% of the time, Pallas kernels for 0%

profile of v3, /device:TPU:1, one launch (start us, length us, event | category | flops | bytes accessed | tf_op | source)
XLA Modules:
  0.0 410.9 jit_solution(16555918140609782002)
XLA Ops:
  7.2 0.0 copy-start
  7.2 0.0 copy-start.7
  7.2 0.0 all-gather.3.cloned.1.call-start
  7.2 0.9 convert_reduce_fusion.1
  8.2 0.7 fusion.91
  8.9 0.7 pad_maximum_fusion.2
  9.5 0.1 copy.26
  9.7 2.3 fusion.22
  11.9 0.0 all-gather.3.cloned.1.call-update
  12.0 0.0 copy-done.7
  12.0 1.8 fusion.52
  13.8 2.3 reshape.202
  16.1 10.5 %all-to-all-start.1 = ((bf16[64,3,4096]{2,1,0:T(4,128)(2,1)}), bf16[64,3,4096]{2,1,0:T(4,128)(2,1)}, u32[]{:S(2)}, u32[]{:S(2)}) async-start(bf16[64,3,4096]{2,1,0:T(4,128)(2,1)} %reshape.202), calls=%async_computation.1 | async-start | bytes 4194304 | tf_op jit(solution)/shard_map/all_to_all | solution.py:53
  26.7 0.0 all-gather.5.cloned.1.call-start
  26.7 49.0 %all-to-all-done.1 = bf16[64,3,4096]{2,1,0:T(4,128)(2,1)} async-done(((bf16[64,3,4096]{2,1,0:T(4,128)(2,1)}), bf16[64,3,4096]{2,1,0:T(4,128)(2,1)}, u32[]{:S(2)}, u32[]{:S(2)}) %all-to-all-start.1) | async-done | bytes 1572896 | tf_op jit(solution)/shard_map/all_to_all | solution.py:53
  75.7 4.3 %reshape.203 = bf16[192,4096]{1,0:T(8,128)(2,1)} reshape(bf16[64,3,4096]{2,1,0:T(4,128)(2,1)} %all-to-all-done.1) | data formatting | bytes 3145728 | tf_op jit(solution)/shard_map/reshape | solution.py:53
  80.0 0.0 all-gather.5.cloned.1.call-update
  80.0 53.1 %all-gather.3.cloned.1.call-done = bf16[1024,4224]{1,0:T(8,128)(2,1)} async-done(((bf16[128,4224]{1,0:T(8,128)(2,1)}), bf16[1024,4224]{1,0:T(8,128)(2,1)}) %all-gather.3.cloned.1.call-update) | async-done | bytes 8650768 | tf_op jit(solution)/shard_map/all_gather | solution.py:51
  133.2 2.4 fusion.39
  135.6 1.2 fusion.49
  136.9 12.3 %fusion.7 = bf16[768,4224]{1,0:T(8,128)(2,1)} fusion(bf16[1024,4224]{1,0:T(8,128)(2,1)} %all-gather.3.cloned.1.call-done, s32[1024]{0:T(1024)S(1)} %fusion.74), kind=kOutput, calls=%fused_computation.15 | convolution fusion | flops 6644563968 | bytes 15142912 | tf_op jit(solution)/shard_map/dot_general | solution.py:18
  149.2 7.6 %all-to-all-start = ((bf16[32,24,4224]{2,1,0:T(8,128)(2,1)}), bf16[32,24,4224]{2,1,0:T(8,128)(2,1)}, u32[]{:S(2)}, u32[]{:S(2)}) async-start(bf16[32,24,4224]{2,1,0:T(8,128)(2,1)} %bitcast.43), calls=%async_computation | async-start | bytes 12976128 | tf_op jit(solution)/shard_map/all_to_all | solution.py:66
  156.7 0.2 reduce-scatter.3.cloned.1.call-start
  157.0 75.4 %all-to-all-done = bf16[32,24,4224]{2,1,0:T(8,128)(2,1)} async-done(((bf16[32,24,4224]{2,1,0:T(8,128)(2,1)}), bf16[32,24,4224]{2,1,0:T(8,128)(2,1)}, u32[]{:S(2)}, u32[]{:S(2)}) %all-to-all-start) | async-done | bytes 6488096 | tf_op jit(solution)/shard_map/all_to_all | solution.py:66
  232.4 1.1 convert_reduce_fusion
  233.5 0.5 select_reduce_fusion
  234.0 0.0 copy-done.2
  234.0 6.0 %fusion.2 = f32[768,384]{1,0:T(8,128)S(1)} fusion(bf16[768,4224]{1,0:T(8,128)(2,1)} %bitcast.4, bf16[192,4096]{1,0:T(8,128)(2,1)} %bitcast.48, bf16[192,4096]{1,0:T(8,128)(2,1)S(1)} %bitcast.45), kind=kOutput, calls=%fused_computation.7 | convolution fusion | flops 2422210560 | bytes 10616832 | tf_op jit(solution)/shard_map/dot_general | solution.py:22
  240.0 3.0 fusion.12
  243.1 6.9 %all-gather.5.cloned.1.call-done = bf16[768,4096]{1,0:T(8,128)(2,1)} async-done(((bf16[192,4096]{1,0:T(8,128)(2,1)}), bf16[768,4096]{1,0:T(8,128)(2,1)}) %all-gather.5.cloned.1.call-update) | async-done | bytes 6291472 | tf_op jit(solution)/shard_map/all_gather | solution.py:68
  250.0 5.4 %multiply_convert_fusion.1 = (bf16[768,192]{0,1:T(8,128)(2,1)S(1)}, bf16[768,192]{0,1:T(8,128)(2,1)S(1)}, bf16[768]{0:T(1024)(128)(2,1)S(1)}) fusion(f32[768]{0:T(1024)S(1)} %select_reduce_fusion, f32[768,384]{0,1:T(8,128)} %fusion.12, bf16[768,4096]{1,0:T(8,128)(2,1)} %all-gather.5.cloned.1.call-done, bf16[1,192,4096]{2,1,0:T(8,128)(2,1)S(1)} %copy-done), kind=kOutput, calls=%fused_computation.60 | convolution fusion | flops 1210465536 | bytes 9638400 | tf_op jit(solution)/shard_map/dot_general | solution.py:22
  255.5 0.0 copy-start.4
  255.5 0.0 copy-start.3
  255.5 1.0 fusion.27
  256.5 0.5 copy-done.3
  257.0 2.7 add_convert_fusion.1
  259.7 0.0 reduce-scatter.3.cloned.1.call-update
  259.7 0.0 reduce-scatter.5.cloned.1.call-start
  259.8 1.0 fusion.9
  260.8 0.7 fusion.10
  261.4 0.0 copy-start.5
  261.5 1.7 fusion.11
  263.2 1.0 fusion.24
  264.2 1.0 add_convert_fusion
  265.3 0.3 pad_maximum_fusion
  265.6 54.8 %all_to_all.20 = bf16[32,24,2176]{2,1,0:T(8,128)(2,1)S(1)} all-to-all(bf16[32,24,2176]{2,1,0:T(8,128)(2,1)S(1)} %bitcast.42), channel_id=1, replica_groups=mesh['seq'=4,'zlo'=2,'y'=4,'x'=4,'core'=2] {'y','x','core'}, dimensions={0} | all-to-all | bytes 6684672 | tf_op jit(solution)/shard_map/all_to_all | solution.py:108
  320.4 5.7 %fusion.8 = bf16[1024,2176]{1,0:T(8,128)(2,1)} fusion(bf16[768,2176]{1,0:T(8,128)(2,1)S(1)} %bitcast.44, s32[1024]{0:T(1024)S(1)} %get-tuple-element.25), kind=kOutput, calls=%fused_computation.16 | convolution fusion | flops 3423338496 | bytes 7802880 | tf_op jit(solution)/shard_map/dot_general | solution.py:18
  326.1 0.0 reduce-scatter.5.cloned.1.call-update
  326.1 6.7 %reduce-scatter.3.cloned.1.call-done = bf16[192,2048]{1,0:T(8,128)(2,1)} async-done(((bf16[768,2048]{1,0:T(8,128)(2,1)}), bf16[192,2048]{1,0:T(8,128)(2,1)}) %reduce-scatter.3.cloned.1.call-update) | async-done | bytes 786448 | tf_op jit(solution)/shard_map/reduce_scatter | solution.py:101
  332.8 3.3 reshape.204
  336.1 8.1 %all-to-all-start.2 = ((bf16[64,3,2048]{2,1,0:T(4,128)(2,1)}), bf16[64,3,2048]{2,1,0:T(4,128)(2,1)S(1)}, u32[]{:S(2)}, u32[]{:S(2)}) async-start(bf16[64,3,2048]{2,1,0:T(4,128)(2,1)} %reshape.204), calls=%async_computation.3 | async-start | bytes 2097152 | tf_op jit(solution)/shard_map/all_to_all | solution.py:112
  344.2 0.0 copy-start.6
  344.2 5.8 %convolution_bitcast_fusion.2 = bf16[1,192,4096]{2,1,0:T(8,128)(2,1)} fusion(bf16[768,192]{0,1:T(8,128)(2,1)S(1)} %fusion.11, bf16[768,4224]{1,0:T(8,128)(2,1)} %bitcast.4), kind=kOutput, calls=%fused_computation.4 | convolution fusion | flops 1207959552 | bytes 8159232 | tf_op jit(solution)/shard_map/dot_general | solution.py:26
  350.0 0.0 copy-done.6
  350.0 5.5 %convolution_bitcast_fusion.1 = bf16[1,192,4096]{2,1,0:T(8,128)(2,1)} fusion(bf16[768,192]{0,1:T(8,128)(2,1)S(1)} %copy-done.6, bf16[768,4224]{1,0:T(8,128)(2,1)} %bitcast.4), kind=kOutput, calls=%fused_computation.3 | convolution fusion | flops 1207959552 | bytes 8159232 | tf_op jit(solution)/shard_map/dot_general | solution.py:26
  355.5 5.6 %convolution_bitcast_fusion = bf16[1,192,4096]{2,1,0:T(8,128)(2,1)} fusion(bf16[768,4096]{1,0:T(8,128)(2,1)} %all-gather.5.cloned.1.call-done, f32[768]{0:T(1024)S(1)} %select_reduce_fusion, f32[768,384]{0,1:T(8,128)S(1)} %copy-done.8), kind=kOutput, calls=%fused_computation.2 | convolution fusion | flops 1208991744 | bytes 9047040 | tf_op jit(solution)/shard_map/dot_general | solution.py:26
  361.0 10.5 %all-to-all-done.2 = bf16[64,3,2048]{2,1,0:T(4,128)(2,1)S(1)} async-done(((bf16[64,3,2048]{2,1,0:T(4,128)(2,1)}), bf16[64,3,2048]{2,1,0:T(4,128)(2,1)S(1)}, u32[]{:S(2)}, u32[]{:S(2)}) %all-to-all-start.2) | async-done | bytes 786464 | tf_op jit(solution)/shard_map/all_to_all | solution.py:112
  371.5 0.7 reshape.205
  372.2 0.3 fusion.50
  372.6 28.3 %reduce-scatter.5.cloned.1.call-done = bf16[128,2176]{1,0:T(8,128)(2,1)} async-done(((bf16[1024,2176]{1,0:T(8,128)(2,1)}), bf16[128,2176]{1,0:T(8,128)(2,1)}) %reduce-scatter.5.cloned.1.call-update) | async-done | bytes 557072 | tf_op jit(solution)/shard_map/reduce_scatter | solution.py:110
  400.9 0.8 slice_convert_fusion
  401.7 0.6 copy.24
  402.3 1.1 slice.53
  403.4 1.1 pad_maximum_fusion.1
  (11 shorter events, 0.1 us)
Async XLA Ops:
  7.2 242.8 %copy-start = (bf16[1,192,4096]{2,1,0:T(8,128)(2,1)S(1)}, bf16[1,192,4096]{2,1,0:T(8,128)(2,1)}, u32[]{:S(2)}) copy-start(bf16[1,192,4096]{2,1,0:T(8,128)(2,1)} %param.12) | copy-start | bytes 4718596
  7.2 4.8 %copy-start.7 = (s32[128,1]{0,1:T(1,128)S(1)}, s32[128,1]{0,1:T(1,128)}, u32[]{:S(2)}) copy-start(s32[128,1]{0,1:T(1,128)} %param.8) | copy-start | bytes 1540
  7.2 126.0 %all-gather.3.cloned.1.call-start = ((), (), s32[]{:S(2)}) async-start(), calls=%async_computation.6 | async-start | bytes 9732096 | tf_op jit(solution)/shard_map/all_gather | solution.py:51
  16.1 59.6 %all-to-all-start.1 = ((bf16[64,3,4096]{2,1,0:T(4,128)(2,1)}), bf16[64,3,4096]{2,1,0:T(4,128)(2,1)}, u32[]{:S(2)}, u32[]{:S(2)}) async-start(bf16[64,3,4096]{2,1,0:T(4,128)(2,1)} %reshape.202), calls=%async_computation.1 | async-start | bytes 4194304 | tf_op jit(solution)/shard_map/all_to_all | solution.py:53
  26.7 223.3 %all-gather.5.cloned.1.call-start = ((), (), s32[]{:S(2)}) async-start(), calls=%async_computation.7 | async-start | bytes 7864320 | tf_op jit(solution)/shard_map/all_gather | solution.py:68
  149.2 84.9 %copy-start.2 = (bf16[1,192,4096]{2,1,0:T(8,128)(2,1)S(1)}, bf16[1,192,4096]{2,1,0:T(8,128)(2,1)}, u32[]{:S(2)}) copy-start(bf16[1,192,4096]{2,1,0:T(8,128)(2,1)} %param.10) | copy-start | bytes 4718596
  149.2 83.2 %all-to-all-start = ((bf16[32,24,4224]{2,1,0:T(8,128)(2,1)}), bf16[32,24,4224]{2,1,0:T(8,128)(2,1)}, u32[]{:S(2)}, u32[]{:S(2)}) async-start(bf16[32,24,4224]{2,1,0:T(8,128)(2,1)} %bitcast.43), calls=%async_computation | async-start | bytes 12976128 | tf_op jit(solution)/shard_map/all_to_all | solution.py:66
  156.7 176.1 %reduce-scatter.3.cloned.1.call-start = ((), (), s32[]{:S(2)}) async-start(), calls=%async_computation.8 | async-start | bytes 3932160 | tf_op jit(solution)/shard_map/reduce_scatter | solution.py:101
  255.5 1.1 copy-start.4
  255.5 1.5 copy-start.3
  259.7 141.2 %reduce-scatter.5.cloned.1.call-start = ((), (), s32[]{:S(2)}) async-start(), calls=%async_computation.9 | async-start | bytes 5013504 | tf_op jit(solution)/shard_map/reduce_scatter | solution.py:110
  261.4 2.8 copy-start.5
  336.1 35.4 %all-to-all-start.2 = ((bf16[64,3,2048]{2,1,0:T(4,128)(2,1)}), bf16[64,3,2048]{2,1,0:T(4,128)(2,1)S(1)}, u32[]{:S(2)}, u32[]{:S(2)}) async-start(bf16[64,3,2048]{2,1,0:T(4,128)(2,1)} %reshape.204), calls=%async_computation.3 | async-start | bytes 2097152 | tf_op jit(solution)/shard_map/all_to_all | solution.py:112
  344.2 5.8 %copy-start.6 = (bf16[768,192]{0,1:T(8,128)(2,1)S(1)}, bf16[768,192]{0,1:T(8,128)(2,1)}, u32[]{:S(2)}) copy-start(bf16[768,192]{0,1:T(8,128)(2,1)} %copy-done.5) | copy-start | bytes 884740
  350.0 5.5 %copy-start.8 = (f32[768,384]{0,1:T(8,128)S(1)}, f32[768,384]{0,1:T(8,128)}, u32[]{:S(2)}) copy-start(f32[768,384]{0,1:T(8,128)} %fusion.12) | copy-start | bytes 3538948
  355.5 48.9 %copy-start.1 = (bf16[1,192,4096]{2,1,0:T(8,128)(2,1)S(1)}, bf16[1,192,4096]{2,1,0:T(8,128)(2,1)}, u32[]{:S(2)}) copy-start(bf16[1,192,4096]{2,1,0:T(8,128)(2,1)} %param.12) | copy-start | bytes 4718596
Sparse Core Ops, SparseCore 0:
  12.1 121.0 all-gather.2
  135.5 114.4 all-gather.4
  259.8 72.9 reduce-scatter.2
  335.3 65.6 reduce-scatter.4
